TPU v7x, 128 devices: a whole 4x4x4 slice. The times are simulated.
128 devices in a mesh: cell: 8 (over z_lo, x), gene: 16 (over z_hi, y, core).
Axes of the slice: x: 4, y: 4, z: 4 (z_hi: 2, z_lo: 2; z = z_hi * 2 + z_lo), core: 2. Of those that a mesh axis runs over, the one named last changes fastest.
Arguments:
- expression: bfloat16 [8192, 30720], P('cell', 'gene'), may hold values from -12 to 12
- prior_values: bfloat16 [30720, 1792], P('gene'), may hold values from -0.0625 to 0.0625
- block_mask: int32 [240, 14], P('gene'), may hold values 0 or 1
- gram_inverse: bfloat16 [1792, 1792], P(None, 'gene'), may hold values from -1 to 2
Outputs:
- coefficients: float32 [1792, 30720], P('cell', 'gene')
All inputs are finite; a program needn't handle non-finite values. No bound on the sum of `block_mask` on one device may be relied on, other than what follows from the above.
Results may differ from a plain program's by a relative error of at most 0.025.
Values may be sent and summed in bfloat16 or wider, within the bound.
A program may use at most 128 MiB of HBM per device.

v0:
```python
import jax
import jax.numpy as jnp
from jax import lax
from jax.sharding import PartitionSpec as P

BLOCK = 128
ITERS = 2


OUT_UNITS = 100.0
LASSO = 0.006
RIDGE = 0.1
PRIOR_RELIEF = 0.7
EPSILON = 1e-06


def shrink(moved, limit, step_size):
    kept = jnp.maximum(moved - limit, 0.0) - jnp.maximum(-moved - limit, 0.0)
    return kept / (1.0 + step_size * RIDGE)


def on_device(expression, prior_values, block_mask, gram_inverse):
    cell_devices = lax.axis_size("cell")
    cell_rows, gene_rows = expression.shape
    tf_total = prior_values.shape[1]
    gene_blocks, tf_blocks = block_mask.shape
    support = block_mask.astype(jnp.bfloat16)[:, None, :, None]
    masked = (prior_values.reshape(gene_blocks, BLOCK, tf_blocks, BLOCK) * support).reshape(
        gene_rows, tf_total
    )
    tf_scores = lax.psum_scatter(
        lax.dot_general(
            masked, expression, (((0,), (1,)), ((), ())), preferred_element_type=jnp.float32
        ).astype(jnp.bfloat16),
        "gene",
        scatter_dimension=0,
        tiled=True,
    )
    activity_part = lax.dot_general(
        gram_inverse,
        lax.all_gather(tf_scores, "gene", axis=0, tiled=True),
        (((0,), (0,)), ((), ())),
        preferred_element_type=jnp.float32,
    ).astype(jnp.bfloat16)
    activity_t = lax.all_gather(activity_part, "gene", axis=0, tiled=True)
    widened = activity_t.astype(jnp.float32)
    sum_squares = lax.psum(jnp.sum(widened * widened), "cell")
    total_cells = cell_rows * cell_devices
    step_size = 0.5 / (sum_squares / (total_cells * tf_total) + EPSILON)
    relief = block_mask.T.astype(jnp.float32)[:, None, :, None]
    penalty = jnp.broadcast_to(1.0 - PRIOR_RELIEF * relief, (tf_blocks, BLOCK, gene_blocks, BLOCK))
    limit = step_size * LASSO * penalty.reshape(tf_total, gene_rows)
    tf_rows = tf_total // cell_devices
    first_row = lax.axis_index("cell") * tf_rows
    coefficient_bf = jnp.zeros((tf_total, gene_rows), jnp.bfloat16)
    coefficient = jnp.zeros((tf_total, gene_rows), jnp.float32)
    for sweep in range(ITERS):
        if sweep == 0:
            residual = -expression
        else:
            fitted = lax.dot_general(
                activity_t,
                coefficient_bf,
                (((0,), (0,)), ((), ())),
                preferred_element_type=jnp.float32,
            )
            residual = (fitted - expression.astype(jnp.float32)).astype(jnp.bfloat16)
        partial_term = jnp.dot(activity_t, residual, preferred_element_type=jnp.float32)
        gradient = (
            lax.psum(partial_term.astype(jnp.bfloat16), "cell").astype(jnp.float32) / total_cells
        )
        coefficient = shrink(coefficient - step_size * gradient, limit, step_size)
        coefficient_bf = coefficient.astype(jnp.bfloat16)
    coefficient = lax.dynamic_slice_in_dim(coefficient, first_row, tf_rows, 0)
    return coefficient * OUT_UNITS


def solution(mesh):
    in_specs = (P("cell", "gene"), P("gene", None), P("gene", None), P(None, "gene"))
    out_specs = P("cell", "gene")
    return jax.shard_map(
        on_device, mesh=mesh, in_specs=in_specs, out_specs=out_specs, check_vma=False
    )
```

profile of v0, /device:TPU:1, one launch (start us, length us, event | category | flops | bytes accessed | tf_op | source)
XLA Modules:
  0.0 598.1 jit_solution(4196749134953552201)
XLA Ops:
  6.5 0.8 convert_element_type.40
  7.3 0.1 copy.6
  7.4 9.8 %copy.7 = bf16[1920,1792]{0,1:T(8,128)(2,1)} copy(bf16[1920,1792]{1,0:T(8,128)(2,1)} %param.5) | data formatting | bytes 13762560 | tf_op args[1]
  17.2 1.0 mul.63
  18.3 1.9 copy-done.3
  20.2 11.3 %fusion.5 = bf16[1792,1024]{1,0:T(8,128)(2,1)} fusion(bf16[1024,1920]{1,0:T(8,128)(2,1)} %param.4, bf16[1920,1792]{0,1:T(8,128)(2,1)S(1)} %copy-done.3, bf16[224,8,15,128]{3,2,1,0:T(8,128)(2,1)S(1)} %bitcast.25), kind=kOutput, calls=%fused_computation.13 | convolution fusion | flops 7051706368 | bytes 21364736 | tf_op jit(solution)/shard_map/dot_general | solution.py:32
  31.5 0.0 reduce-scatter.2.cloned.1.call-update
  31.5 0.0 all-gather.3.cloned.1.call-start
  31.6 79.6 %reduce-scatter.2.cloned.1.call-done = bf16[112,1024]{1,0:T(8,128)(2,1)} async-done(((bf16[1792,1024]{1,0:T(8,128)(2,1)}), bf16[112,1024]{1,0:T(8,128)(2,1)}) %reduce-scatter.2.cloned.1.call-update) | async-done | bytes 229392 | tf_op jit(solution)/shard_map/reduce_scatter | solution.py:31
  111.2 0.0 all-gather.3.cloned.1.call-update
  111.2 0.0 all-gather.5.cloned.1.call-start
  111.2 56.9 %all-gather.3.cloned.1.call-done = bf16[1792,1024]{1,0:T(8,128)(2,1)} async-done(((bf16[112,1024]{1,0:T(8,128)(2,1)}), bf16[1792,1024]{1,0:T(8,128)(2,1)}) %all-gather.3.cloned.1.call-update) | async-done | bytes 3670032 | tf_op jit(solution)/shard_map/all_gather | solution.py:41
  168.1 3.4 fusion.6
  171.5 0.0 all-gather.5.cloned.1.call-update
  171.5 0.0 all-reduce.3.cloned.1.call-start
  171.6 52.9 %all-gather.5.cloned.1.call-done = bf16[1792,1024]{1,0:T(8,128)(2,1)} async-done(((bf16[112,1024]{1,0:T(8,128)(2,1)}), bf16[1792,1024]{1,0:T(8,128)(2,1)}) %all-gather.5.cloned.1.call-update) | async-done | bytes 3670032 | tf_op jit(solution)/shard_map/all_gather | solution.py:45
  224.5 12.5 %convolution_convert_fusion.1 = bf16[1792,1920]{1,0:T(8,128)(2,1)} fusion(bf16[1792,1024]{1,0:T(8,128)(2,1)} %all-gather.5.cloned.1.call-done, bf16[1024,1920]{1,0:T(8,128)(2,1)} %param.4), kind=kOutput, calls=%fused_computation.5 | convolution fusion | flops 7051837440 | bytes 14483456 | tf_op jit(solution)/shard_map/dot_general | solution.py:68
  236.9 0.0 all-reduce.3.cloned.1.call-update
  237.0 0.0 all-reduce.5.cloned.1.call-start
  237.0 4.5 multiply_reduce_fusion
  241.6 18.2 %psum.22 = f32[]{:T(128)} all-reduce(f32[]{:T(128)} %multiply_reduce_fusion), channel_id=1, replica_groups=mesh['cell'=8,'gene'=16] {'cell'}, use_global_device_ids=true, to_apply=%region_3.0 | all-reduce | flops 1 | bytes 8 | tf_op jit(solution)/shard_map/psum | solution.py:47
  260.5 0.1 copy.8
  260.6 130.6 %all-reduce.3.cloned.1.call-done = bf16[1792,1920]{1,0:T(8,128)(2,1)} async-done(((bf16[1792,1920]{1,0:T(8,128)(2,1)}), bf16[1792,1920]{1,0:T(8,128)(2,1)}) %all-reduce.3.cloned.1.call-update) | async-done | bytes 6881296 | tf_op jit(solution)/shard_map/psum | solution.py:70
  391.2 1.0 broadcast_in_dim.2
  392.2 1.9 copy-done.2
  394.1 13.1 %subtract_divide_fusion = (f32[1792,1920]{1,0:T(8,128)}, f32[1792,1920]{1,0:T(8,128)}) fusion(bf16[1792,1920]{1,0:T(8,128)(2,1)S(1)} %copy-done.2, f32[]{:T(128)S(6)} %add.19, f32[]{:T(128)S(6)} %mul.67, f32[224,8,15,128]{3,2,1,0:T(8,128)S(1)} %bitcast.24), kind=kLoop, calls=%fused_computation.2 | loop fusion | flops 34406400 | bytes 48168968 | tf_op jit(solution)/shard_map/div | solution.py:19
  407.2 11.8 %fusion.2 = f32[1024,1920]{1,0:T(8,128)S(1)} fusion(bf16[1792,1024]{1,0:T(8,128)(2,1)S(1)} %copy-done.4, f32[1792,1920]{1,0:T(8,128)} %get-tuple-element.5), kind=kOutput, calls=%fused_computation.10 | convolution fusion | flops 7049871360 | bytes 25296896 | tf_op jit(solution)/shard_map/dot_general | solution.py:61
  419.0 9.9 %convolution_convert_fusion = bf16[1792,1920]{1,0:T(8,128)(2,1)} fusion(bf16[1792,1024]{1,0:T(8,128)(2,1)S(1)} %copy-done.4, f32[1024,1920]{1,0:T(8,128)S(1)} %fusion.2, bf16[1024,1920]{1,0:T(8,128)(2,1)S(1)} %copy-done.6), kind=kOutput, calls=%fused_computation.4 | convolution fusion | flops 7055769600 | bytes 22347776 | tf_op jit(solution)/shard_map/dot_general | solution.py:68
  428.9 0.0 all-reduce.5.cloned.1.call-update
  428.9 154.9 %all-reduce.5.cloned.1.call-done = bf16[1792,1920]{1,0:T(8,128)(2,1)} async-done(((bf16[1792,1920]{1,0:T(8,128)(2,1)}), bf16[1792,1920]{1,0:T(8,128)(2,1)}) %all-reduce.5.cloned.1.call-update) | async-done | bytes 6881296 | tf_op jit(solution)/shard_map/psum | solution.py:70
  583.9 3.9 convert_multiply_fusion
  587.8 3.8 divide_multiply_fusion
  (14 shorter events, 0.0 us)
Async XLA Ops:
  6.5 161.6 %copy-start = (bf16[1792,112]{0,1:T(8,128)(2,1)S(1)}, bf16[1792,112]{0,1:T(8,128)(2,1)}, u32[]{:S(2)}) copy-start(bf16[1792,112]{0,1:T(8,128)(2,1)} %param.7) | copy-start | bytes 1204228
  6.5 104.6 %reduce-scatter.2.cloned.1.call-start = ((), (), s32[]{:S(2)}) async-start(), calls=%async_computation.1 | async-start | bytes 3899392 | tf_op jit(solution)/shard_map/reduce_scatter | solution.py:31
  17.2 3.0 copy-start.3
  31.5 136.6 %all-gather.3.cloned.1.call-start = ((), (), s32[]{:S(2)}) async-start(), calls=%async_computation.2 | async-start | bytes 3899392 | tf_op jit(solution)/shard_map/all_gather | solution.py:41
  111.2 113.3 %all-gather.5.cloned.1.call-start = ((), (), s32[]{:S(2)}) async-start(), calls=%async_computation.3 | async-start | bytes 3899392 | tf_op jit(solution)/shard_map/all_gather | solution.py:45
  171.5 219.6 %all-reduce.3.cloned.1.call-start = ((), (), s32[]{:S(2)}) async-start(), calls=%async_computation.4 | async-start | bytes 13762560 | tf_op jit(solution)/shard_map/psum | solution.py:70
  236.9 23.5 %copy-start.5 = (s32[15,14]{1,0:T(8,128)S(1)}, s32[15,14]{1,0:T(8,128)}, u32[]{:S(2)}) copy-start(s32[15,14]{1,0:T(8,128)} %param.6) | copy-start | bytes 2524
  237.0 346.9 %all-reduce.5.cloned.1.call-start = ((), (), s32[]{:S(2)}) async-start(), calls=%async_computation.5 | async-start | bytes 13762560 | tf_op jit(solution)/shard_map/psum | solution.py:70
  391.2 3.0 copy-start.2
  394.1 13.1 %copy-start.4 = (bf16[1792,1024]{1,0:T(8,128)(2,1)S(1)}, bf16[1792,1024]{1,0:T(8,128)(2,1)}, u32[]{:S(2)}) copy-start(bf16[1792,1024]{1,0:T(8,128)(2,1)} %all-gather.5.cloned.1.call-done) | copy-start | bytes 11010052
  407.2 11.8 %copy-start.6 = (bf16[1024,1920]{1,0:T(8,128)(2,1)S(1)}, bf16[1024,1920]{1,0:T(8,128)(2,1)}, u32[]{:S(2)}) copy-start(bf16[1024,1920]{1,0:T(8,128)(2,1)} %param.4) | copy-start | bytes 11796484
  583.9 7.7 %copy-start.1 = (bf16[1792,112]{0,1:T(8,128)(2,1)S(1)}, bf16[1792,112]{0,1:T(8,128)(2,1)}, u32[]{:S(2)}) copy-start(bf16[1792,112]{0,1:T(8,128)(2,1)} %param.7) | copy-start | bytes 1204228
Sparse Core Ops, SparseCore 0:
  31.7 79.4 reduce-scatter.1
  113.6 54.4 all-gather.2
  171.7 52.7 all-gather.4
  237.1 154.0 all-reduce.2
  429.1 154.7 all-reduce.4
where the time goes:
time: 599 us; the launch traced here: 598 us
  waiting for transfers between devices  475 us (79%)
  matrix products  48.9 us (8%)
  other arithmetic  26 us (4%)
  blocking collectives  18.2 us (3%)
  local copies, waits for them, and re-layouts  15.9 us (3%)
  between operations  13.9 us (2%)
    psum x2, waiting for transfers between devices, on_device(): lax.psum(partial_term.astype(jnp.bfloat16), 'cell').astype(jnp.float32)  286 us
    reduce_scatter x1, waiting for transfers between devices, on_device(): lax.psum_scatter(lax.dot_general(masked, expression, (((0,), (1,)), ((),...  79.6 us
    all_gather x1, waiting for transfers between devices, on_device(): lax.all_gather(tf_scores, 'gene', axis=0, tiled=True)  56.9 us
    all_gather x1, waiting for transfers between devices, on_device(): activity_t = lax.all_gather(activity_part, 'gene', axis=0, tiled=True)  52.9 us
    dot_general x2, matrix products, on_device(): jnp.dot(activity_t, residual, preferred_element_type=jnp.float32)  22.4 us
    psum x1, blocking collectives, on_device(): sum_squares = lax.psum(jnp.sum(widened * widened), 'cell')  18.2 us
    unnamed x15, local copies, waits for them, and re-layouts  13.7 us
    div x1, other arithmetic, shrink(): return kept / (1.0 + step_size * RIDGE)  13.1 us
  transfers between devices with their start and end apart: 5, of which 5 were waited for; matrix products, arithmetic and copies ran while one was open for 1% of the time, Pallas kernels for 0%

commit v1 on v0

--- a/solution.py
+++ b/solution.py
@@ -4,8 +4,6 @@
 from jax.sharding import PartitionSpec as P
 
 BLOCK = 128
-ITERS = 2
-
 
 OUT_UNITS = 100.0
 LASSO = 0.006
@@ -47,31 +45,34 @@
     sum_squares = lax.psum(jnp.sum(widened * widened), "cell")
     total_cells = cell_rows * cell_devices
     step_size = 0.5 / (sum_squares / (total_cells * tf_total) + EPSILON)
+    tf_rows = tf_total // cell_devices
+    first_row = lax.axis_index("cell") * tf_rows
     relief = block_mask.T.astype(jnp.float32)[:, None, :, None]
     penalty = jnp.broadcast_to(1.0 - PRIOR_RELIEF * relief, (tf_blocks, BLOCK, gene_blocks, BLOCK))
-    limit = step_size * LASSO * penalty.reshape(tf_total, gene_rows)
-    tf_rows = tf_total // cell_devices
-    first_row = lax.axis_index("cell") * tf_rows
-    coefficient_bf = jnp.zeros((tf_total, gene_rows), jnp.bfloat16)
-    coefficient = jnp.zeros((tf_total, gene_rows), jnp.float32)
-    for sweep in range(ITERS):
-        if sweep == 0:
-            residual = -expression
-        else:
-            fitted = lax.dot_general(
-                activity_t,
-                coefficient_bf,
-                (((0,), (0,)), ((), ())),
-                preferred_element_type=jnp.float32,
-            )
-            residual = (fitted - expression.astype(jnp.float32)).astype(jnp.bfloat16)
-        partial_term = jnp.dot(activity_t, residual, preferred_element_type=jnp.float32)
-        gradient = (
-            lax.psum(partial_term.astype(jnp.bfloat16), "cell").astype(jnp.float32) / total_cells
-        )
-        coefficient = shrink(coefficient - step_size * gradient, limit, step_size)
-        coefficient_bf = coefficient.astype(jnp.bfloat16)
-    coefficient = lax.dynamic_slice_in_dim(coefficient, first_row, tf_rows, 0)
+    penalty = lax.dynamic_slice_in_dim(penalty.reshape(tf_total, gene_rows), first_row, tf_rows, 0)
+    limit = step_size * LASSO * penalty
+
+    gram_part = lax.dot_general(
+        activity_t,
+        activity_part,
+        (((1,), (1,)), ((), ())),
+        preferred_element_type=jnp.float32,
+    ).astype(jnp.bfloat16)
+    first_term = jnp.dot(activity_t, expression, preferred_element_type=jnp.float32)
+    first = lax.psum_scatter(
+        first_term.astype(jnp.bfloat16), "cell", scatter_dimension=0, tiled=True
+    ).astype(jnp.float32)
+    gram_rows = lax.all_gather(
+        lax.psum_scatter(gram_part, "cell", scatter_dimension=0, tiled=True),
+        "gene",
+        axis=1,
+        tiled=True,
+    )
+    scale = step_size / total_cells
+    coefficient = shrink(scale * first, limit, step_size)
+    whole = lax.all_gather(coefficient.astype(jnp.bfloat16), "cell", axis=0, tiled=True)
+    second = jnp.dot(gram_rows, whole, preferred_element_type=jnp.float32)
+    coefficient = shrink(coefficient - scale * (second - first), limit, step_size)
     return coefficient * OUT_UNITS
 
 

time: 599 us -> 448 us (0.75)
  waiting for transfers between devices: 475 us -> 296 us
  blocking collectives: 18.2 us -> 52.4 us
  local copies, waits for them, and re-layouts: 15.9 us -> 37.9 us
  other arithmetic: 26 us -> 7.81 us
  matrix products: 48.9 us -> 38.4 us
    psum x2 -> x0, waiting for transfers between devices: 286 us -> none  [on_device(): lax.psum(partial_term.astype(jnp.bfloat16), 'cell').astype(jnp.float32)]
    reduce_scatter x0 -> x2, waiting for transfers between devices: none -> 56.2 us  [the longest x1 30.7 us: on_device(): lax.psum_scatter(gram_part, 'cell', scatter_dimension=0, tiled=True)]
    all_gather x0 -> x1, waiting for transfers between devices: none -> 50.8 us  [on_device(): lax.all_gather(coefficient.astype(jnp.bfloat16), 'cell', axis=0, tiled=True)]
    all_gather x0 -> x1, blocking collectives: none -> 34.2 us  [on_device(): lax.all_gather(lax.psum_scatter(gram_part, 'cell', scatter_dimension=0, t...]
    unnamed x15 -> x14, local copies, waits for them, and re-layouts: 13.7 us -> 29.5 us
    div x1 -> x0, other arithmetic: 13.1 us -> none  [shrink(): return kept / (1.0 + step_size * RIDGE)]
    dot_general x3, matrix products: 34.2 us -> 23.7 us  [the longest x1 12.3 us: on_device(): jnp.dot(activity_t, expression, preferred_element_type=jnp.float32)]
    mul x3 -> x0, other arithmetic: 7.66 us -> none  [the longest x1 3.89 us: on_device(): coefficient = shrink(coefficient - step_size * gradient, limit, step_size)]
  transfers between devices with their start and end apart: 5 -> 6, of which waited for: 5 -> 6; matrix products, arithmetic and copies ran while one was open for 1% -> 8% of each run, Pallas kernels for 0% -> 0%
where the time goes in v1:
time: 448 us
  waiting for transfers between devices  296 us (66%)
  blocking collectives  52.4 us (12%)
  matrix products  38.4 us (9%)
  local copies, waits for them, and re-layouts  37.9 us (8%)
  between operations  14.2 us (3%)
  other arithmetic  7.81 us (2%)
    reduce_scatter x1, waiting for transfers between devices, on_device(): lax.psum_scatter(lax.dot_general(masked, expression, (((0,), (1,)), ((),...  79.6 us
    all_gather x1, waiting for transfers between devices, on_device(): lax.all_gather(tf_scores, 'gene', axis=0, tiled=True)  56.8 us
    all_gather x1, waiting for transfers between devices, on_device(): activity_t = lax.all_gather(activity_part, 'gene', axis=0, tiled=True)  52.9 us
    all_gather x1, waiting for transfers between devices, on_device(): lax.all_gather(coefficient.astype(jnp.bfloat16), 'cell', axis=0, tiled=True)  50.8 us
    all_gather x1, blocking collectives, on_device(): lax.all_gather(lax.psum_scatter(gram_part, 'cell', scatter_dimension=0, t...  34.2 us
    reduce_scatter x1, waiting for transfers between devices, on_device(): lax.psum_scatter(gram_part, 'cell', scatter_dimension=0, tiled=True)  30.7 us
    unnamed x14, local copies, waits for them, and re-layouts  29.5 us
    reduce_scatter x1, waiting for transfers between devices, on_device(): lax.psum_scatter(first_term.astype(jnp.bfloat16), 'cell', scatter_dimensi...  25.5 us
  transfers between devices with their start and end apart: 6, of which 6 were waited for; matrix products, arithmetic and copies ran while one was open for 8% of the time, Pallas kernels for 0%

profile of v1, /device:TPU:1, one launch (start us, length us, event | category | flops | bytes accessed | tf_op | source)
XLA Modules:
  0.0 447.6 jit_solution(2163153683050519931)
XLA Ops:
  6.5 10.0 %copy.10 = bf16[1920,1792]{0,1:T(8,128)(2,1)} copy(bf16[1920,1792]{1,0:T(8,128)(2,1)} %param.5) | data formatting | bytes 13762560 | tf_op args[1]
  16.5 0.1 copy.9
  16.6 1.0 mul.54
  17.7 1.9 copy-done.2
  19.6 11.3 %fusion.2 = bf16[1792,1024]{1,0:T(8,128)(2,1)} fusion(bf16[1024,1920]{1,0:T(8,128)(2,1)} %param.4, bf16[1920,1792]{0,1:T(8,128)(2,1)S(1)} %copy-done.2, bf16[224,8,15,128]{3,2,1,0:T(8,128)(2,1)S(1)} %bitcast.29), kind=kOutput, calls=%fused_computation.6 | convolution fusion | flops 7051706368 | bytes 21364736 | tf_op jit(solution)/shard_map/dot_general | solution.py:30
  30.9 0.0 reduce-scatter.4.cloned.1.call-update
  30.9 0.0 all-gather.4.cloned.1.call-start
  31.0 79.6 %reduce-scatter.4.cloned.1.call-done = bf16[112,1024]{1,0:T(8,128)(2,1)} async-done(((bf16[1792,1024]{1,0:T(8,128)(2,1)}), bf16[112,1024]{1,0:T(8,128)(2,1)}) %reduce-scatter.4.cloned.1.call-update) | async-done | bytes 229392 | tf_op jit(solution)/shard_map/reduce_scatter | solution.py:29
  110.6 0.0 all-gather.4.cloned.1.call-update
  110.6 0.0 all-gather.6.cloned.1.call-start
  110.7 56.8 %all-gather.4.cloned.1.call-done = bf16[1792,1024]{1,0:T(8,128)(2,1)} async-done(((bf16[112,1024]{1,0:T(8,128)(2,1)}), bf16[1792,1024]{1,0:T(8,128)(2,1)}) %all-gather.4.cloned.1.call-update) | async-done | bytes 3670032 | tf_op jit(solution)/shard_map/all_gather | solution.py:39
  167.5 3.4 convolution_convert_fusion.2
  170.9 0.0 reduce-scatter.6.cloned.1.call-start
  171.0 52.9 %all-gather.6.cloned.1.call-done = bf16[1792,1024]{1,0:T(8,128)(2,1)} async-done(((bf16[112,1024]{1,0:T(8,128)(2,1)}), bf16[1792,1024]{1,0:T(8,128)(2,1)}) %all-gather.6.cloned.1.call-update) | async-done | bytes 3670032 | tf_op jit(solution)/shard_map/all_gather | solution.py:43
  223.9 12.3 %convolution_convert_fusion = bf16[1792,1920]{1,0:T(8,128)(2,1)} fusion(bf16[1792,1024]{1,0:T(8,128)(2,1)} %all-gather.6.cloned.1.call-done, bf16[1024,1920]{1,0:T(8,128)(2,1)} %param.4), kind=kOutput, calls=%fused_computation.1 | convolution fusion | flops 7049871360 | bytes 14483456 | tf_op jit(solution)/shard_map/dot_general | solution.py:61
  236.2 0.0 reduce-scatter.6.cloned.1.call-update
  236.2 0.2 reduce-scatter.8.cloned.1.call-start
  236.4 0.1 copy.11
  236.5 6.2 %broadcast_in_dim.2 = f32[14,128,15,128]{3,2,1,0:T(8,128)} broadcast(f32[14,15]{1,0:T(8,128)S(1)} %copy.11), dimensions={0,2} | broadcast | bytes 13763400 | tf_op jit(solution)/shard_map/broadcast_in_dim | solution.py:51
  242.7 17.6 %copy.22 = f32[224,8,15,128]{3,1,2,0:T(8,128)} copy(f32[224,8,15,128]{3,2,1,0:T(8,128)} %bitcast.26) | data formatting | bytes 27525120
  260.3 3.9 convolution_convert_fusion.1
  264.3 0.0 reduce-scatter.8.cloned.1.call-update
  264.3 0.0 all-gather.8.cloned.1.call-start
  264.4 4.6 %multiply_reduce_fusion = f32[]{:T(128)} fusion(bf16[1792,1024]{1,0:T(8,128)(2,1)} %all-gather.6.cloned.1.call-done), kind=kLoop, calls=%fused_computation.2 | loop fusion | flops 5505023 | bytes 3670020 | tf_op jit(solution)/shard_map/reduce_sum | solution.py:45
  268.9 18.2 %psum.7 = f32[]{:T(128)} all-reduce(f32[]{:T(128)} %multiply_reduce_fusion), channel_id=1, replica_groups=mesh['cell'=8,'gene'=16] {'cell'}, use_global_device_ids=true, to_apply=%region_2.0 | all-reduce | flops 1 | bytes 8 | tf_op jit(solution)/shard_map/psum | solution.py:45
  287.9 25.5 %reduce-scatter.6.cloned.1.call-done = bf16[224,1920]{1,0:T(8,128)(2,1)} async-done(((bf16[1792,1920]{1,0:T(8,128)(2,1)}), bf16[224,1920]{1,0:T(8,128)(2,1)}) %reduce-scatter.6.cloned.1.call-update) | async-done | bytes 860176 | tf_op jit(solution)/shard_map/reduce_scatter | solution.py:62
  313.3 3.2 fusion.12
  316.6 30.7 %reduce-scatter.8.cloned.1.call-done = bf16[224,112]{1,0:T(8,128)(2,1)} async-done(((bf16[1792,112]{1,0:T(8,128)(2,1)}), bf16[224,112]{1,0:T(8,128)(2,1)}) %reduce-scatter.8.cloned.1.call-update) | async-done | bytes 50192 | tf_op jit(solution)/shard_map/reduce_scatter | solution.py:66
  347.3 0.9 copy.12
  348.2 34.2 %all_gather.14 = bf16[224,1792]{0,1:T(8,128)(2,1)S(1)} all-gather(bf16[224,112]{0,1:T(8,128)(2,1)S(1)} %copy.12), channel_id=1, replica_groups=mesh['cell'=8,'gene'=16] {'gene'}, dimensions={1}, use_global_device_ids=true | all-gather | bytes 852992 | tf_op jit(solution)/shard_map/all_gather | solution.py:65
  382.4 50.8 %all-gather.8.cloned.1.call-done = bf16[1792,1920]{1,0:T(8,128)(2,1)} async-done(((bf16[224,1920]{1,0:T(8,128)(2,1)}), bf16[1792,1920]{1,0:T(8,128)(2,1)}) %all-gather.8.cloned.1.call-update) | async-done | bytes 6881296 | tf_op jit(solution)/shard_map/all_gather | solution.py:73
  433.3 7.5 %divide_multiply_fusion = f32[224,1920]{1,0:T(8,128)} fusion(bf16[224,1920]{1,0:T(8,128)(2,1)S(1)} %copy-done.4, bf16[224,1792]{0,1:T(8,128)(2,1)S(1)} %all_gather.14, bf16[1792,1920]{1,0:T(8,128)(2,1)} %all-gather.8.cloned.1.call-done, f32[1792,1920]{1,0:T(8,128)} %bitcast.28, s32[]{:T(128)S(6)} %select_n.3, f32[]{:T(128)S(6)} %add.20, f32[]{:T(128)S(6)} %mul.60, ...), kind=kOutput, calls=%fused_computation.19 | convolution fusion | flops 1550438400 | bytes 11984912 | tf_op jit(solution)/shard_map/dot_general | solution.py:74
  (16 shorter events, 0.1 us)
Async XLA Ops:
  6.5 161.0 %copy-start = (bf16[1792,112]{0,1:T(8,128)(2,1)S(1)}, bf16[1792,112]{0,1:T(8,128)(2,1)}, u32[]{:S(2)}) copy-start(bf16[1792,112]{0,1:T(8,128)(2,1)} %param.7) | copy-start | bytes 1204228
  6.5 10.0 %copy-start.5 = (s32[15,14]{1,0:T(8,128)S(1)}, s32[15,14]{1,0:T(8,128)}, u32[]{:S(2)}) copy-start(s32[15,14]{1,0:T(8,128)} %param.6) | copy-start | bytes 2524
  6.5 104.1 %reduce-scatter.4.cloned.1.call-start = ((), (), s32[]{:S(2)}) async-start(), calls=%async_computation.3 | async-start | bytes 3899392 | tf_op jit(solution)/shard_map/reduce_scatter | solution.py:29
  16.6 3.0 copy-start.2
  30.9 136.6 %all-gather.4.cloned.1.call-start = ((), (), s32[]{:S(2)}) async-start(), calls=%async_computation.4 | async-start | bytes 3899392 | tf_op jit(solution)/shard_map/all_gather | solution.py:39
  110.6 113.2 %all-gather.6.cloned.1.call-start = ((), (), s32[]{:S(2)}) async-start(), calls=%async_computation.5 | async-start | bytes 3899392 | tf_op jit(solution)/shard_map/all_gather | solution.py:43
  170.9 142.4 %reduce-scatter.6.cloned.1.call-start = ((), (), s32[]{:S(2)}) async-start(), calls=%async_computation.6 | async-start | bytes 7741440 | tf_op jit(solution)/shard_map/reduce_scatter | solution.py:62
  236.2 111.1 %reduce-scatter.8.cloned.1.call-start = ((), (), s32[]{:S(2)}) async-start(), calls=%async_computation.7 | async-start | bytes 516096 | tf_op jit(solution)/shard_map/reduce_scatter | solution.py:66
  242.7 17.6 %copy-start.3 = (bf16[1024,112]{0,1:T(8,128)(2,1)S(1)}, bf16[1024,112]{0,1:T(8,128)(2,1)}, u32[]{:S(2)}) copy-start(bf16[1024,112]{0,1:T(8,128)(2,1)} %convolution_convert_fusion.2) | copy-start | bytes 688132
  264.3 169.0 %all-gather.8.cloned.1.call-start = ((), (), s32[]{:S(2)}) async-start(), calls=%async_computation.8 | async-start | bytes 7741440 | tf_op jit(solution)/shard_map/all_gather | solution.py:73
  313.3 119.9 %copy-start.4 = (bf16[224,1920]{1,0:T(8,128)(2,1)S(1)}, bf16[224,1920]{1,0:T(8,128)(2,1)}, u32[]{:S(2)}) copy-start(bf16[224,1920]{1,0:T(8,128)(2,1)} %reduce-scatter.6.cloned.1.call-done) | copy-start | bytes 2580484
  433.3 7.5 %copy-start.1 = (bf16[1792,112]{0,1:T(8,128)(2,1)S(1)}, bf16[1792,112]{0,1:T(8,128)(2,1)}, u32[]{:S(2)}) copy-start(bf16[1792,112]{0,1:T(8,128)(2,1)} %param.7) | copy-start | bytes 1204228
Sparse Core Ops, SparseCore 0:
  31.1 79.5 reduce-scatter.3
  113.0 54.4 all-gather.3
  171.0 52.7 all-gather.5
  236.3 76.9 reduce-scatter.5
  315.5 31.7 reduce-scatter.7
  348.8 84.4 all-gather.7

commit v2 on v1

--- a/solution.py
+++ b/solution.py
@@ -1,6 +1,10 @@
+import functools
+
 import jax
 import jax.numpy as jnp
 from jax import lax
+from jax.experimental import pallas as pl
+from jax.experimental.pallas import tpu as pltpu
 from jax.sharding import PartitionSpec as P
 
 BLOCK = 128
@@ -11,10 +15,204 @@
 PRIOR_RELIEF = 0.7
 EPSILON = 1e-06
 
+MESH = pl.DeviceIdType.MESH
+CHIPS = 8
+CHUNK = 256
+OFFSETS = ((0, 1), (0, 3), (1, 0), (0, 2), (1, 1), (1, 3), (1, 2))
+
 
 def shrink(moved, limit, step_size):
     kept = jnp.maximum(moved - limit, 0.0) - jnp.maximum(-moved - limit, 0.0)
     return kept / (1.0 + step_size * RIDGE)
+
+
+def activity_kernel(
+    x_hbm, prior_hbm, support_ref, gram_ref, at_ref,
+    x, prior, part, pair, total, got, scores, acc,
+    x_sem, prior_sem, pair_send, pair_recv, rs_send, rs_recv,
+    ag_send, ag_recv, fw_send, fw_recv, at_send, at_recv, af_send, af_recv,
+):
+    chunks = prior.shape[0]
+    me = lax.axis_index("gene")
+    core = me % 2
+    chip = me // 2
+    y, z = chip % 4, chip // 4
+    partner = chip * 2 + (1 - core)
+    others = [((z + dz) % 2) * 4 + (y + dy) % 4 for dz, dy in OFFSETS]
+
+    x_copy = pltpu.make_async_copy(x_hbm, x, x_sem)
+    x_copy.start()
+
+    def prior_copy(n):
+        columns = pl.ds(pl.multiple_of(n * CHUNK, CHUNK), CHUNK)
+        return pltpu.make_async_copy(prior_hbm.at[:, columns], prior.at[n], prior_sem.at[n])
+
+    for n in range(chunks):
+        prior_copy(n).start()
+
+    barrier = pltpu.get_barrier_semaphore()
+    for device in [other * 2 + core for other in others] + [partner]:
+        pl.semaphore_signal(barrier, inc=1, device_id={"gene": device}, device_id_type=MESH)
+    pl.semaphore_wait(barrier, len(others) + 1)
+
+    def remote(src, dst, send, recv, device):
+        return pltpu.make_async_remote_copy(
+            src_ref=src, dst_ref=dst, send_sem=send, recv_sem=recv,
+            device_id={"gene": device}, device_id_type=MESH,
+        )
+
+    def pair_copy(n):
+        return remote(
+            part.at[n, :, 1 - core], pair.at[n], pair_send.at[n], pair_recv.at[n], partner
+        )
+
+    def rs_copy(n, o, slot):
+        return remote(
+            total.at[n, others[o]], got.at[n, slot], rs_send.at[n, o], rs_recv.at[n, slot],
+            others[o] * 2 + core,
+        )
+
+    def ag_copy(n, o, slot):
+        block = scores.at[n, slot, core]
+        return remote(block, block, ag_send.at[n, o], ag_recv.at[n, slot], others[o] * 2 + core)
+
+    def fw_copy(n, slot, side):
+        block = scores.at[n, slot, side]
+        return remote(block, block, fw_send.at[n, slot], fw_recv.at[n, slot], partner)
+
+    def at_copy(o, slot):
+        block = at_ref.at[slot * 2 + core]
+        return remote(block, block, at_send.at[o], at_recv.at[slot], others[o] * 2 + core)
+
+    def af_copy(slot, side):
+        block = at_ref.at[slot * 2 + side]
+        return remote(block, block, af_send.at[slot], af_recv.at[slot], partner)
+
+    x_copy.wait()
+
+    def spread(n):
+        pair_copy(n).wait_recv()
+        own = part[n, :, core].astype(jnp.float32)
+        total[n] = (own + pair[n].astype(jnp.float32)).astype(jnp.bfloat16)
+        for o in range(len(others)):
+            rs_copy(n, o, chip).start()
+
+    def multiply(n, carry):
+        prior_copy(n).wait()
+        masked = prior[n].reshape(-1, BLOCK // 16, 16, CHUNK) * support_ref[n][:, None]
+        prior[n] = masked.reshape(prior.shape[1:])
+        product = jnp.dot(x[...], prior[n], preferred_element_type=jnp.float32)
+        part[n] = product.astype(jnp.bfloat16).reshape(part.shape[1:])
+        pair_copy(n).start()
+
+        @pl.when(n > 0)
+        def _():
+            spread(n - 1)
+
+        return carry
+
+    lax.fori_loop(0, chunks, multiply, 0)
+    spread(chunks - 1)
+
+    def collect(n, carry):
+        value = total[n, chip].astype(jnp.float32)
+        for o in range(len(others)):
+            rs_copy(n, o, others[o]).wait_recv()
+            value = value + got[n, others[o]].astype(jnp.float32)
+        scores[n, chip, core] = value.astype(jnp.bfloat16)
+        for o in range(len(others)):
+            ag_copy(n, o, chip).start()
+        fw_copy(n, chip, core).start()
+        return carry
+
+    lax.fori_loop(0, chunks, collect, 0)
+
+    def forward(n, carry):
+        for o in range(len(others)):
+            ag_copy(n, o, others[o]).wait_recv()
+            fw_copy(n, others[o], core).start()
+        return carry
+
+    lax.fori_loop(0, chunks, forward, 0)
+
+    acc[...] = jnp.zeros_like(acc)
+
+    def mix(n, carry):
+        for slot in range(CHIPS):
+            fw_copy(n, slot, 1 - core).wait_recv()
+        acc[...] += lax.dot_general(
+            gram_ref[n], scores[n].reshape(-1, CHUNK), (((1,), (1,)), ((), ())),
+            preferred_element_type=jnp.float32,
+        )
+        return carry
+
+    lax.fori_loop(0, chunks, mix, 0)
+    at_ref[me] = acc[...].astype(jnp.bfloat16)
+    for o in range(len(others)):
+        at_copy(o, chip).start()
+    af_copy(chip, core).start()
+    for o in range(len(others)):
+        at_copy(o, others[o]).wait_recv()
+        af_copy(others[o], core).start()
+    for slot in range(CHIPS):
+        af_copy(slot, 1 - core).wait_recv()
+
+    def drain(n, carry):
+        pair_copy(n).wait_send()
+        for o in range(len(others)):
+            rs_copy(n, o, chip).wait_send()
+            ag_copy(n, o, chip).wait_send()
+        for slot in range(CHIPS):
+            fw_copy(n, slot, core).wait_send()
+        return carry
+
+    lax.fori_loop(0, chunks, drain, 0)
+    for o in range(len(others)):
+        at_copy(o, chip).wait_send()
+    for slot in range(CHIPS):
+        af_copy(slot, core).wait_send()
+
+
+def activity_of(expression, prior_values, block_mask, gram_inverse):
+    devices = lax.axis_size("gene")
+    cells, genes = expression.shape
+    factors = prior_values.shape[1]
+    own = gram_inverse.shape[1]
+    chunks = factors // CHUNK
+    rows = cells // devices
+    support = jnp.repeat(block_mask.astype(jnp.bfloat16), BLOCK, axis=1)
+    support = support.reshape(genes // BLOCK, chunks, 1, CHUNK).transpose(1, 0, 2, 3)
+    support = jnp.broadcast_to(support, (chunks, genes // BLOCK, 16, CHUNK))
+    gram = gram_inverse.T.reshape(own, chunks, CHUNK).transpose(1, 0, 2)
+    bf = jnp.bfloat16
+    dma = pltpu.SemaphoreType.DMA
+    links = len(OFFSETS)
+    return pl.pallas_call(
+        activity_kernel,
+        out_shape=jax.ShapeDtypeStruct((devices, own, cells), bf),
+        in_specs=[pl.BlockSpec(memory_space=pl.ANY)] * 2
+        + [pl.BlockSpec(memory_space=pltpu.VMEM)] * 2,
+        out_specs=pl.BlockSpec(memory_space=pltpu.VMEM),
+        scratch_shapes=[
+            pltpu.VMEM((cells, genes), bf),
+            pltpu.VMEM((chunks, genes, CHUNK), bf),
+            pltpu.VMEM((chunks, CHIPS, 2, rows, CHUNK), bf),
+            pltpu.VMEM((chunks, CHIPS, rows, CHUNK), bf),
+            pltpu.VMEM((chunks, CHIPS, rows, CHUNK), bf),
+            pltpu.VMEM((chunks, CHIPS, rows, CHUNK), bf),
+            pltpu.VMEM((chunks, CHIPS, 2, rows, CHUNK), bf),
+            pltpu.VMEM((own, cells), jnp.float32),
+            dma, dma((chunks,)), dma((chunks,)), dma((chunks,)),
+            dma((chunks, links)), dma((chunks, CHIPS)),
+            dma((chunks, links)), dma((chunks, CHIPS)),
+            dma((chunks, CHIPS)), dma((chunks, CHIPS)),
+            dma((links,)), dma((CHIPS,)), dma((CHIPS,)), dma((CHIPS,)),
+        ],
+        compiler_params=pltpu.CompilerParams(
+            collective_id=0, has_side_effects=True, vmem_limit_bytes=56 * 2**20
+        ),
+        name="activity",
+    )(expression, prior_values, support, gram)
 
 
 def on_device(expression, prior_values, block_mask, gram_inverse):
@@ -22,25 +220,9 @@
     cell_rows, gene_rows = expression.shape
     tf_total = prior_values.shape[1]
     gene_blocks, tf_blocks = block_mask.shape
-    support = block_mask.astype(jnp.bfloat16)[:, None, :, None]
-    masked = (prior_values.reshape(gene_blocks, BLOCK, tf_blocks, BLOCK) * support).reshape(
-        gene_rows, tf_total
-    )
-    tf_scores = lax.psum_scatter(
-        lax.dot_general(
-            masked, expression, (((0,), (1,)), ((), ())), preferred_element_type=jnp.float32
-        ).astype(jnp.bfloat16),
-        "gene",
-        scatter_dimension=0,
-        tiled=True,
-    )
-    activity_part = lax.dot_general(
-        gram_inverse,
-        lax.all_gather(tf_scores, "gene", axis=0, tiled=True),
-        (((0,), (0,)), ((), ())),
-        preferred_element_type=jnp.float32,
-    ).astype(jnp.bfloat16)
-    activity_t = lax.all_gather(activity_part, "gene", axis=0, tiled=True)
+    blocks = activity_of(expression, prior_values, block_mask, gram_inverse)
+    activity_part = lax.dynamic_index_in_dim(blocks, lax.axis_index("gene"), 0, keepdims=False)
+    activity_t = blocks.reshape(tf_total, cell_rows)
     widened = activity_t.astype(jnp.float32)
     sum_squares = lax.psum(jnp.sum(widened * widened), "cell")
     total_cells = cell_rows * cell_devices

time: 448 us -> 325 us (0.73)
  waiting for transfers between devices: 296 us -> 109 us
  Pallas kernels: 0 us -> 89.6 us
  matrix products: 38.4 us -> 23 us
  local copies, waits for them, and re-layouts: 37.9 us -> 27.3 us
    all_gather x2 -> x0, waiting for transfers between devices: 110 us -> none  [the longest x1 56.8 us: on_device(): lax.all_gather(tf_scores, 'gene', axis=0, tiled=True)]
    pallas_call x0 -> x1, Pallas kernels: none -> 89.6 us  [activity_of(): pl.pallas_call(activity_kernel, out_shape=jax.ShapeDtypeStruct((devices,...]
    reduce_scatter x1 -> x0, waiting for transfers between devices: 79.6 us -> none  [on_device(): lax.psum_scatter(lax.dot_general(masked, expression, (((0,), (1,)), ((),...]
    dot_general x2 -> x0, matrix products: 14.7 us -> none  [the longest x1 11.3 us: on_device(): lax.dot_general(masked, expression, (((0,), (1,)), ((), ())), preferred_e...]
    unnamed x14 -> x7, local copies, waits for them, and re-layouts: 29.5 us -> 17.2 us
  transfers between devices with their start and end apart: 6 -> 3, of which waited for: 6 -> 3; matrix products, arithmetic and copies ran while one was open for 8% -> 11% of each run, Pallas kernels for 0% -> 0%
where the time goes in v2:
time: 325 us; the launch traced here: 324 us
  waiting for transfers between devices  109 us (34%)
  Pallas kernels  89.6 us (28%)
  blocking collectives  53 us (16%)
  local copies, waits for them, and re-layouts  27.3 us (8%)
  matrix products  23 us (7%)
  between operations  13.9 us (4%)
  other arithmetic  8.4 us (3%)
    pallas_call x1, Pallas kernels, activity_of(): pl.pallas_call(activity_kernel, out_shape=jax.ShapeDtypeStruct((devices,...  89.6 us
    all_gather x1, waiting for transfers between devices, on_device(): lax.all_gather(coefficient.astype(jnp.bfloat16), 'cell', axis=0, tiled=True)  51.2 us
    all_gather x1, blocking collectives, on_device(): lax.all_gather(lax.psum_scatter(gram_part, 'cell', scatter_dimension=0, t...  34 us
    reduce_scatter x1, waiting for transfers between devices, on_device(): lax.psum_scatter(gram_part, 'cell', scatter_dimension=0, tiled=True)  30.9 us
    reduce_scatter x1, waiting for transfers between devices, on_device(): lax.psum_scatter(first_term.astype(jnp.bfloat16), 'cell', scatter_dimensi...  26.8 us
    psum x1, blocking collectives, on_device(): sum_squares = lax.psum(jnp.sum(widened * widened), 'cell')  19 us
    unnamed x7, local copies, waits for them, and re-layouts  17.2 us
    dot_general x1, matrix products, on_device(): jnp.dot(activity_t, expression, preferred_element_type=jnp.float32)  11.7 us
  transfers between devices with their start and end apart: 3, of which 3 were waited for; matrix products, arithmetic and copies ran while one was open for 11% of the time, Pallas kernels for 0%

profile of v2, /device:TPU:1, one launch (start us, length us, event | category | flops | bytes accessed | tf_op | source)
XLA Modules:
  0.0 324.3 jit_solution(15378621373379261058)
XLA Ops:
  6.5 0.0 reduce-scatter.3.cloned.1.call-start
  6.5 0.7 convert_element_type.23
  7.2 0.1 broadcast_in_dim.16
  7.4 1.8 copy.18
  9.2 1.0 broadcast_in_dim.18.support_ref
  10.1 0.0 copy-start
  10.2 89.6 %activity.1 = bf16[16,112,1024]{2,1,0:T(8,128)(2,1)} custom-call(bf16[1024,1920]{1,0:T(8,128)(2,1)} %x_hbm.1, bf16[1920,1792]{1,0:T(8,128)(2,1)} %prior_hbm.1, bf16[7,15,16,256]{3,2,1,0:T(8,128)(2,1)} %broadcast_in_dim.18.support_ref, bf16[7,112,256]{2,1,0:T(8,128)(2,1)} %bitcast.32), custom_call_target="tpu_custom_call" | custom-call | tf_op jit(solution)/shard_map/activity/pallas_call | solution.py:190
  99.7 0.0 copy-done
  99.7 11.7 %convolution_convert_fusion = bf16[1792,1920]{1,0:T(8,128)(2,1)} fusion(bf16[1792,1024]{1,0:T(8,128)(2,1)} %bitcast.30, bf16[1024,1920]{1,0:T(8,128)(2,1)S(1)} %copy-done), kind=kOutput, calls=%fused_computation.1 | convolution fusion | flops 7049871360 | bytes 14483456 | tf_op jit(solution)/shard_map/dot_general | solution.py:243
  111.5 0.0 reduce-scatter.3.cloned.1.call-update
  111.5 0.0 reduce-scatter.5.cloned.1.call-start
  111.5 3.9 %convolution_convert_fusion.1 = bf16[1792,112]{1,0:T(8,128)(2,1)} fusion(bf16[1792,1024]{1,0:T(8,128)(2,1)} %bitcast.31, bf16[16,112,1024]{2,1,0:T(8,128)(2,1)} %activity.1, s32[]{:T(128)S(6)} %select_n.8), kind=kOutput, calls=%fused_computation.6 | convolution fusion | flops 411242496 | bytes 4300804 | tf_op jit(solution)/shard_map/dot_general | solution.py:237
  115.5 0.0 reduce-scatter.5.cloned.1.call-update
  115.5 0.0 copy-start.2
  115.5 0.0 all-gather.2.cloned.1.call-start
  115.5 4.5 %multiply_reduce_fusion = f32[]{:T(128)} fusion(bf16[16,112,1024]{2,1,0:T(8,128)(2,1)} %activity.1), kind=kLoop, calls=%fused_computation.2 | loop fusion | flops 5505023 | bytes 3670020 | tf_op jit(solution)/shard_map/reduce_sum | solution.py:227
  120.1 19.0 %psum.7 = f32[]{:T(128)} all-reduce(f32[]{:T(128)} %multiply_reduce_fusion), channel_id=1, replica_groups=mesh['cell'=8,'gene'=16] {'cell'}, use_global_device_ids=true, to_apply=%region_1.2 | all-reduce | flops 1 | bytes 8 | tf_op jit(solution)/shard_map/psum | solution.py:227
  139.1 0.0 copy-done.2
  139.1 0.1 copy.11
  139.2 6.2 %broadcast_in_dim.19 = f32[14,128,15,128]{3,2,1,0:T(8,128)} broadcast(f32[14,15]{1,0:T(8,128)S(1)} %copy.11), dimensions={0,2} | broadcast | bytes 13763400 | tf_op jit(solution)/shard_map/broadcast_in_dim | solution.py:233
  145.4 17.2 %copy.17 = f32[224,8,15,128]{3,1,2,0:T(8,128)} copy(f32[224,8,15,128]{3,2,1,0:T(8,128)} %bitcast.27) | data formatting | bytes 27525120
  163.3 26.8 %reduce-scatter.3.cloned.1.call-done = bf16[224,1920]{1,0:T(8,128)(2,1)} async-done(((bf16[1792,1920]{1,0:T(8,128)(2,1)}), bf16[224,1920]{1,0:T(8,128)(2,1)}) %reduce-scatter.3.cloned.1.call-update) | async-done | bytes 860176 | tf_op jit(solution)/shard_map/reduce_scatter | solution.py:244
  190.1 3.2 fusion.12
  193.3 0.0 copy-start.1
  193.3 0.0 all-gather.2.cloned.1.call-update
  193.3 30.9 %reduce-scatter.5.cloned.1.call-done = bf16[224,112]{1,0:T(8,128)(2,1)} async-done(((bf16[1792,112]{1,0:T(8,128)(2,1)}), bf16[224,112]{1,0:T(8,128)(2,1)}) %reduce-scatter.5.cloned.1.call-update) | async-done | bytes 50192 | tf_op jit(solution)/shard_map/reduce_scatter | solution.py:248
  224.2 0.9 copy.12
  225.2 34.0 %all_gather.6 = bf16[224,1792]{0,1:T(8,128)(2,1)S(1)} all-gather(bf16[224,112]{0,1:T(8,128)(2,1)S(1)} %copy.12), channel_id=1, replica_groups=mesh['cell'=8,'gene'=16] {'gene'}, dimensions={1}, use_global_device_ids=true | all-gather | bytes 852992 | tf_op jit(solution)/shard_map/all_gather | solution.py:247
  259.1 51.2 %all-gather.2.cloned.1.call-done = bf16[1792,1920]{1,0:T(8,128)(2,1)} async-done(((bf16[224,1920]{1,0:T(8,128)(2,1)}), bf16[1792,1920]{1,0:T(8,128)(2,1)}) %all-gather.2.cloned.1.call-update) | async-done | bytes 6881296 | tf_op jit(solution)/shard_map/all_gather | solution.py:255
  310.4 0.0 copy-done.1
  310.4 7.4 %divide_multiply_fusion = f32[224,1920]{1,0:T(8,128)} fusion(bf16[224,1920]{1,0:T(8,128)(2,1)S(1)} %copy-done.1, bf16[224,1792]{0,1:T(8,128)(2,1)S(1)} %all_gather.6, bf16[1792,1920]{1,0:T(8,128)(2,1)} %all-gather.2.cloned.1.call-done, f32[1792,1920]{1,0:T(8,128)} %bitcast.29, s32[]{:T(128)S(6)} %select_n.7, f32[]{:T(128)S(6)} %add.22, f32[]{:T(128)S(6)} %mul.47, ...), kind=kOutput, calls=%fused_computation.15 | convolution fusion | flops 1550438400 | bytes 11984912 | tf_op jit(solution)/shard_map/dot_general | solution.py:256
  (3 shorter events, 0.0 us)
Async XLA Ops:
  6.5 183.6 %reduce-scatter.3.cloned.1.call-start = ((), (), s32[]{:S(2)}) async-start(), calls=%async_computation.2 | async-start | bytes 7741440 | tf_op jit(solution)/shard_map/reduce_scatter | solution.py:244
  10.1 89.6 %copy-start = (bf16[1024,1920]{1,0:T(8,128)(2,1)S(1)}, bf16[1024,1920]{1,0:T(8,128)(2,1)}, u32[]{:S(2)}) copy-start(bf16[1024,1920]{1,0:T(8,128)(2,1)} %x_hbm.1) | copy-start | bytes 11796484
  111.5 112.8 %reduce-scatter.5.cloned.1.call-start = ((), (), s32[]{:S(2)}) async-start(), calls=%async_computation.3 | async-start | bytes 516096 | tf_op jit(solution)/shard_map/reduce_scatter | solution.py:248
  115.5 23.6 %copy-start.2 = (s32[15,14]{1,0:T(8,128)S(1)}, s32[15,14]{1,0:T(8,128)}, u32[]{:S(2)}) copy-start(s32[15,14]{1,0:T(8,128)} %param.6) | copy-start | bytes 2524
  115.5 194.9 %all-gather.2.cloned.1.call-start = ((), (), s32[]{:S(2)}) async-start(), calls=%async_computation.4 | async-start | bytes 7741440 | tf_op jit(solution)/shard_map/all_gather | solution.py:255
  193.3 117.1 %copy-start.1 = (bf16[224,1920]{1,0:T(8,128)(2,1)S(1)}, bf16[224,1920]{1,0:T(8,128)(2,1)}, u32[]{:S(2)}) copy-start(bf16[224,1920]{1,0:T(8,128)(2,1)} %reduce-scatter.3.cloned.1.call-done) | copy-start | bytes 2580484
Sparse Core Ops, SparseCore 0:
  111.6 78.4 reduce-scatter.2
  192.5 31.7 reduce-scatter.4
  225.9 84.4 all-gather.1

commit v3 on v2

--- a/solution.py
+++ b/solution.py
@@ -19,11 +19,6 @@
 CHIPS = 8
 CHUNK = 256
 OFFSETS = ((0, 1), (0, 3), (1, 0), (0, 2), (1, 1), (1, 3), (1, 2))
-
-
-def shrink(moved, limit, step_size):
-    kept = jnp.maximum(moved - limit, 0.0) - jnp.maximum(-moved - limit, 0.0)
-    return kept / (1.0 + step_size * RIDGE)
 
 
 def activity_kernel(
@@ -215,47 +210,373 @@
     )(expression, prior_values, support, gram)
 
 
+Z_ROWS = 1024
+HOPS = 4
+
+
+def solve_kernel(
+    at_ref, x_hbm, relief_ref, out_ref,
+    x, part, z1, zs, x1, x2, xs, z2, gram_part, gram_got, gram, squares, penalty,
+    first, coef, coef_bf, sent,
+    x_sem, z1_send, z1_recv, x1_send, x1_recv, x2_send, x2_recv, z2_send, z2_recv,
+    gp_send, gp_recv, gc_send, gc_recv, gg_send, gg_recv, gf_send, gf_recv,
+    sq_send, sq_recv, out_send, out_recv,
+):
+    cells = 2 * HOPS
+    pieces = gram_part.shape[0]
+    factors, width = first.shape
+    cell, gene = lax.axis_index("cell"), lax.axis_index("gene")
+    x_at, z_lo = cell % HOPS, cell // HOPS
+    core, y_at, z_hi = gene % 2, (gene // 2) % 4, gene // 8
+    z_partner = (1 - z_lo) * HOPS + x_at
+    core_partner = z_hi * 8 + y_at * 2 + (1 - core)
+    near = [(cell, z_hi * 8 + ((y_at + dy) % 4) * 2 + core) for dy in (1, 3, 2)]
+    near += [(z_partner, (1 - z_hi) * 8 + ((y_at + dy) % 4) * 2 + core) for dy in (0, 1, 3, 2)]
+
+    def remote(src, dst, send, recv, at_cell, at_gene):
+        return pltpu.make_async_remote_copy(
+            src_ref=src, dst_ref=dst, send_sem=send, recv_sem=recv,
+            device_id={"cell": at_cell, "gene": at_gene}, device_id_type=MESH,
+        )
+
+    tail = x_hbm.shape[1] - (cells - 1) * width
+
+    def x_copy(d):
+        lanes = tail if d == cells - 1 else width
+        return pltpu.make_async_copy(
+            x_hbm.at[:, pl.ds(d * width, lanes)], x.at[d, :, pl.ds(0, lanes)], x_sem.at[d]
+        )
+
+    for d in range(cells):
+        x_copy(d).start()
+    x[cells - 1, :, tail:] = jnp.zeros((x.shape[1], width - tail), x.dtype)
+
+    barrier = pltpu.get_barrier_semaphore()
+    greeted = [((cell + o) % cells, gene) for o in range(1, cells)]
+    greeted += near + [(cell, core_partner)]
+    for at_cell, at_gene in greeted:
+        pl.semaphore_signal(
+            barrier, inc=1, device_id={"cell": at_cell, "gene": at_gene}, device_id_type=MESH
+        )
+    pl.semaphore_wait(barrier, len(greeted))
+
+    whole = at_ref[...].reshape(factors, -1)
+    product = lax.dot_general(
+        at_ref[gene], whole, (((1,), (1,)), ((), ())), preferred_element_type=jnp.float32
+    )
+    gram_part[...] = product.astype(jnp.bfloat16).reshape(gram_part.shape)
+
+    def gp_copy(r, slot):
+        return remote(gram_part.at[r], gram_got.at[slot], gp_send.at[r], gp_recv.at[slot], r, gene)
+
+    for r in range(pieces):
+        @pl.when(cell != r)
+        def _():
+            gp_copy(r, cell).start()
+
+    for d in range(cells):
+        x_copy(d).wait()
+
+    def z1_copy(x_to):
+        d = (1 - z_lo) * HOPS + x_to
+        return remote(
+            part.at[d, pl.ds(0, Z_ROWS)], z1.at[x_to], z1_send.at[x_to], z1_recv.at[x_to],
+            z_partner, gene,
+        )
+
+    rest = pl.ds(Z_ROWS, factors - Z_ROWS)
+
+    def x1_copy(z_to, x_to, slot):
+        return remote(
+            part.at[z_to * HOPS + x_to, rest], x1.at[slot, z_to],
+            x1_send.at[x_to, z_to], x1_recv.at[slot, z_to], z_lo * HOPS + x_to, gene,
+        )
+
+    def x2_copy(x_to, slot):
+        return remote(
+            zs.at[x_to], x2.at[slot], x2_send.at[x_to], x2_recv.at[slot],
+            z_lo * HOPS + x_to, gene,
+        )
+
+    def z2_copy():
+        return remote(xs, z2, z2_send, z2_recv, z_partner, gene)
+
+    def multiply(i, carry):
+        x_to = (x_at + 1 + i) % HOPS
+        z_to = (z_lo + 1 + i // HOPS) % 2
+        d = z_to * HOPS + x_to
+        value = jnp.dot(
+            at_ref[...].reshape(factors, -1), x[d], preferred_element_type=jnp.float32
+        )
+        part[d] = value.astype(jnp.bfloat16)
+
+        @pl.when(i < HOPS)
+        def _():
+            z1_copy(x_to).start()
+
+        @pl.when(x_to != x_at)
+        def _():
+            x1_copy(z_to, x_to, x_at).start()
+
+        return carry
+
+    lax.fori_loop(0, cells, multiply, 0)
+
+    def gc_copy(t, r):
+        block = gram.at[gene, r]
+        return remote(block, block, gc_send.at[t], gc_recv.at[r], t, gene)
+
+    for r in range(pieces):
+        @pl.when(cell == r)
+        def _():
+            value = gram_part[r].astype(jnp.float32)
+            for o in range(1, cells):
+                slot = (cell + o) % cells
+                gp_copy(r, slot).wait_recv()
+                value = value + gram_got[slot].astype(jnp.float32)
+            gram[gene, r] = value.astype(jnp.bfloat16)
+            for o in range(1, cells):
+                gc_copy((cell + o) % cells, r).start()
+
+    def sq_copy(t, slot):
+        return remote(squares.at[slot], squares.at[slot], sq_send.at[t], sq_recv.at[slot], t, gene)
+
+    def square(b, total):
+        value = at_ref[b].astype(jnp.float32)
+        return total + jnp.sum((value * value).reshape(-1, 8, value.shape[1]), axis=0)
+
+    squares[cell] = lax.fori_loop(
+        0, at_ref.shape[0], square, jnp.zeros(squares.shape[1:], jnp.float32)
+    )
+    for o in range(1, cells):
+        sq_copy((cell + o) % cells, cell).start()
+
+    for b in range(relief_ref.shape[0]):
+        rows = jnp.broadcast_to(relief_ref[b][None], (BLOCK // 8, 8, width))
+        penalty[pl.ds(b * BLOCK, BLOCK)] = rows.reshape(BLOCK, width)
+
+    def pair_sum(i):
+        x_to = (x_at + 1 + i) % HOPS
+        z1_copy(x_to).wait_recv()
+        own = part[z_lo * HOPS + x_to, :Z_ROWS].astype(jnp.float32)
+        zs[x_to] = (own + z1[x_to].astype(jnp.float32)).astype(jnp.bfloat16)
+        if i < HOPS - 1:
+            x2_copy(x_to, x_at).start()
+
+    pair_sum(0)
+
+    def gg_copy(k, slot):
+        at_cell, at_gene = near[k]
+        return remote(
+            gram.at[slot], gram.at[slot], gg_send.at[k], gg_recv.at[slot], at_cell, at_gene
+        )
+
+    def gf_copy(slot):
+        return remote(
+            gram.at[slot], gram.at[slot], gf_send.at[slot // 2], gf_recv.at[slot], cell, core_partner
+        )
+
+    for r in range(pieces):
+        @pl.when(cell != r)
+        def _():
+            gc_copy(cell, r).wait_recv()
+
+    for k in range(len(near)):
+        gg_copy(k, gene).start()
+    gf_copy(gene).start()
+
+    def forward(k):
+        slot = near[k][1]
+        gg_copy(k, slot).wait_recv()
+        gf_copy(slot).start()
+
+    pair_sum(1)
+    pair_sum(2)
+
+    value = part[(1 - z_lo) * HOPS + x_at, Z_ROWS:].astype(jnp.float32)
+    for o in range(1, HOPS):
+        slot = (x_at + o) % HOPS
+        x1_copy(1 - z_lo, x_at, slot).wait_recv()
+        value = value + x1[slot, 1 - z_lo].astype(jnp.float32)
+    xs[...] = value.astype(jnp.bfloat16)
+    z2_copy().start()
+
+    pair_sum(3)
+
+    for k in range(len(near)):
+        forward(k)
+
+    for o in range(1, cells):
+        sq_copy(cell, (cell + o) % cells).wait_recv()
+    sum_squares = jnp.sum(jnp.sum(squares[...], axis=0), keepdims=True)
+    total_cells = cells * x.shape[1]
+    step_size = 0.5 / (sum_squares / (total_cells * factors) + EPSILON)
+    scale = step_size / total_cells
+    inverse = 1.0 / (1.0 + step_size * RIDGE)
+
+    def shrunk(moved, rows):
+        limit = step_size * penalty[rows]
+        return (jnp.maximum(moved - limit, 0.0) - jnp.maximum(-moved - limit, 0.0)) * inverse
+
+    def start_from(value, rows):
+        first[rows] = value
+        start = shrunk(scale * value, rows)
+        coef[rows] = start
+        coef_bf[rows] = start.astype(jnp.bfloat16)
+
+    for o in range(1, HOPS):
+        slot = (x_at + o) % HOPS
+        x2_copy(x_at, slot).wait_recv()
+        x1_copy(z_lo, x_at, slot).wait_recv()
+
+    def z_block(b, carry):
+        rows = pl.ds(pl.multiple_of(b * BLOCK, BLOCK), BLOCK)
+        value = zs[x_at, rows].astype(jnp.float32)
+        for o in range(1, HOPS):
+            value = value + x2[(x_at + o) % HOPS, rows].astype(jnp.float32)
+        start_from(value, rows)
+        return carry
+
+    lax.fori_loop(0, Z_ROWS // BLOCK, z_block, 0)
+    z2_copy().wait_recv()
+
+    def x_block(b, carry):
+        low = pl.ds(pl.multiple_of(b * BLOCK, BLOCK), BLOCK)
+        rows = pl.ds(pl.multiple_of(b * BLOCK + Z_ROWS, BLOCK), BLOCK)
+        value = part[cell, rows].astype(jnp.float32) + z2[low].astype(jnp.float32)
+        for o in range(1, HOPS):
+            value = value + x1[(x_at + o) % HOPS, z_lo, low].astype(jnp.float32)
+        start_from(value, rows)
+        return carry
+
+    lax.fori_loop(0, (factors - Z_ROWS) // BLOCK, x_block, 0)
+
+    gf_slots = [n * 2 + 1 - core for n in range(gram.shape[0] // 2)]
+    for slot in gf_slots:
+        gf_copy(slot).wait_recv()
+
+    height = out_ref.shape[1]
+
+    def out_copy(t, slot):
+        return remote(sent.at[t], out_ref.at[slot], out_send.at[t], out_recv.at[slot], t, gene)
+
+    def finish(i, carry):
+        t = (cell + 1 + i) % cells
+        rows = pl.ds(pl.multiple_of(t * height, 32), height)
+        block = gram[pl.ds(t * 2, 2)].reshape(height, factors)
+        second = jnp.dot(block, coef_bf[...], preferred_element_type=jnp.float32)
+        moved = coef[rows] - scale * (second - first[rows])
+        value = (shrunk(moved, rows) * OUT_UNITS).astype(jnp.bfloat16)
+
+        @pl.when(i < cells - 1)
+        def _():
+            sent[t] = value
+            out_copy(t, cell).start()
+
+        @pl.when(i == cells - 1)
+        def _():
+            out_ref[cell] = value
+
+        return carry
+
+    lax.fori_loop(0, cells, finish, 0)
+
+    for r in range(pieces):
+        @pl.when(cell != r)
+        def _():
+            gp_copy(r, cell).wait_send()
+
+        @pl.when(cell == r)
+        def _():
+            for o in range(1, cells):
+                gc_copy((cell + o) % cells, r).wait_send()
+
+    for x_to in range(HOPS):
+        z1_copy(x_to).wait_send()
+    for o in range(1, HOPS):
+        x_to = (x_at + o) % HOPS
+        x2_copy(x_to, x_at).wait_send()
+        for z_to in range(2):
+            x1_copy(z_to, x_to, x_at).wait_send()
+    z2_copy().wait_send()
+    for k in range(len(near)):
+        gg_copy(k, gene).wait_send()
+    for n in range(gram.shape[0] // 2):
+        gf_copy(n * 2 + core).wait_send()
+    for o in range(1, cells):
+        t = (cell + o) % cells
+        sq_copy(t, cell).wait_send()
+        out_copy(t, cell).wait_send()
+        out_copy(cell, t).wait_recv()
+
+
+def solve(activity_t, expression, block_mask):
+    cell_devices, gene_devices = lax.axis_size("cell"), lax.axis_size("gene")
+    _, own, cells = activity_t.shape
+    factors = gene_devices * own
+    width = CHUNK
+    gene_blocks, tf_blocks = block_mask.shape
+    per = width // BLOCK
+    relief = jnp.pad(block_mask.T.astype(jnp.float32), ((0, 0), (0, cell_devices * per - gene_blocks)))
+    relief = lax.dynamic_slice_in_dim(relief, lax.axis_index("cell") * per, per, 1)
+    relief = jnp.repeat(LASSO * (1.0 - PRIOR_RELIEF * relief), BLOCK, axis=1)
+    relief = jnp.broadcast_to(relief[:, None], (tf_blocks, 8, width))
+    pieces = own // 16
+    rest = factors - Z_ROWS
+    bf, f32 = jnp.bfloat16, jnp.float32
+    vmem, dma = pltpu.VMEM, pltpu.SemaphoreType.DMA
+    return pl.pallas_call(
+        solve_kernel,
+        out_shape=jax.ShapeDtypeStruct((cell_devices, factors // cell_devices, width), bf),
+        in_specs=[
+            pl.BlockSpec(memory_space=pltpu.VMEM),
+            pl.BlockSpec(memory_space=pl.ANY),
+            pl.BlockSpec(memory_space=pltpu.VMEM),
+        ],
+        out_specs=pl.BlockSpec(memory_space=pltpu.VMEM),
+        scratch_shapes=[
+            vmem((cell_devices, cells, width), bf),
+            vmem((cell_devices, factors, width), bf),
+            vmem((HOPS, Z_ROWS, width), bf),
+            vmem((HOPS, Z_ROWS, width), bf),
+            vmem((HOPS, 2, rest, width), bf),
+            vmem((HOPS, Z_ROWS, width), bf),
+            vmem((rest, width), bf),
+            vmem((rest, width), bf),
+            vmem((pieces, 16, factors), bf),
+            vmem((cell_devices, 16, factors), bf),
+            vmem((gene_devices, pieces, 16, factors), bf),
+            vmem((cell_devices, 8, cells), f32),
+            vmem((factors, width), f32),
+            vmem((factors, width), f32),
+            vmem((factors, width), f32),
+            vmem((factors, width), bf),
+            vmem((cell_devices, factors // cell_devices, width), bf),
+            dma((cell_devices,)),
+            dma((HOPS,)), dma((HOPS,)),
+            dma((HOPS, 2)), dma((HOPS, 2)),
+            dma((HOPS,)), dma((HOPS,)),
+            dma, dma,
+            dma((pieces,)), dma((cell_devices,)),
+            dma((cell_devices,)), dma((pieces,)),
+            dma((7,)), dma((gene_devices,)),
+            dma((gene_devices // 2,)), dma((gene_devices,)),
+            dma((cell_devices,)), dma((cell_devices,)),
+            dma((cell_devices,)), dma((cell_devices,)),
+        ],
+        compiler_params=pltpu.CompilerParams(
+            collective_id=1, has_side_effects=True, vmem_limit_bytes=60 * 2**20
+        ),
+        name="solve",
+    )(activity_t, expression, relief)
+
+
 def on_device(expression, prior_values, block_mask, gram_inverse):
-    cell_devices = lax.axis_size("cell")
-    cell_rows, gene_rows = expression.shape
-    tf_total = prior_values.shape[1]
-    gene_blocks, tf_blocks = block_mask.shape
-    blocks = activity_of(expression, prior_values, block_mask, gram_inverse)
-    activity_part = lax.dynamic_index_in_dim(blocks, lax.axis_index("gene"), 0, keepdims=False)
-    activity_t = blocks.reshape(tf_total, cell_rows)
-    widened = activity_t.astype(jnp.float32)
-    sum_squares = lax.psum(jnp.sum(widened * widened), "cell")
-    total_cells = cell_rows * cell_devices
-    step_size = 0.5 / (sum_squares / (total_cells * tf_total) + EPSILON)
-    tf_rows = tf_total // cell_devices
-    first_row = lax.axis_index("cell") * tf_rows
-    relief = block_mask.T.astype(jnp.float32)[:, None, :, None]
-    penalty = jnp.broadcast_to(1.0 - PRIOR_RELIEF * relief, (tf_blocks, BLOCK, gene_blocks, BLOCK))
-    penalty = lax.dynamic_slice_in_dim(penalty.reshape(tf_total, gene_rows), first_row, tf_rows, 0)
-    limit = step_size * LASSO * penalty
-
-    gram_part = lax.dot_general(
-        activity_t,
-        activity_part,
-        (((1,), (1,)), ((), ())),
-        preferred_element_type=jnp.float32,
-    ).astype(jnp.bfloat16)
-    first_term = jnp.dot(activity_t, expression, preferred_element_type=jnp.float32)
-    first = lax.psum_scatter(
-        first_term.astype(jnp.bfloat16), "cell", scatter_dimension=0, tiled=True
-    ).astype(jnp.float32)
-    gram_rows = lax.all_gather(
-        lax.psum_scatter(gram_part, "cell", scatter_dimension=0, tiled=True),
-        "gene",
-        axis=1,
-        tiled=True,
-    )
-    scale = step_size / total_cells
-    coefficient = shrink(scale * first, limit, step_size)
-    whole = lax.all_gather(coefficient.astype(jnp.bfloat16), "cell", axis=0, tiled=True)
-    second = jnp.dot(gram_rows, whole, preferred_element_type=jnp.float32)
-    coefficient = shrink(coefficient - scale * (second - first), limit, step_size)
-    return coefficient * OUT_UNITS
+    activity_t = activity_of(expression, prior_values, block_mask, gram_inverse)
+    blocks = solve(activity_t, expression, block_mask)
+    rows = blocks.shape[1]
+    whole = blocks.transpose(1, 0, 2).reshape(rows, -1)
+    return whole[:, : expression.shape[1]].astype(jnp.float32)
 
 
 def solution(mesh):

time: 325 us -> 226 us (0.70)
  Pallas kernels: 89.6 us -> 218 us
  waiting for transfers between devices: 109 us -> 0 us
  blocking collectives: 53 us -> 0 us
  matrix products: 23 us -> 0 us
  local copies, waits for them, and re-layouts: 27.3 us -> 5 us
  between operations: 13.9 us -> 0.08 us
  other arithmetic: 8.4 us -> 2.11 us
    pallas_call x0 -> x1, Pallas kernels: none -> 129 us  [solve(): pl.pallas_call(solve_kernel, out_shape=jax.ShapeDtypeStruct((cell_devices...]
    reduce_scatter x2 -> x0, waiting for transfers between devices: 57.7 us -> none  [the longest x1 30.9 us: on_device(): lax.psum_scatter(gram_part, 'cell', scatter_dimension=0, tiled=True)]
    all_gather x1 -> x0, waiting for transfers between devices: 51.2 us -> none  [on_device(): lax.all_gather(coefficient.astype(jnp.bfloat16), 'cell', axis=0, tiled=True)]
    all_gather x1 -> x0, blocking collectives: 34 us -> none  [on_device(): lax.all_gather(lax.psum_scatter(gram_part, 'cell', scatter_dimension=0, t...]
    dot_general x3 -> x0, matrix products: 23 us -> none  [the longest x1 11.7 us: on_device(): jnp.dot(activity_t, expression, preferred_element_type=jnp.float32)]
    psum x1 -> x0, blocking collectives: 19 us -> none  [on_device(): sum_squares = lax.psum(jnp.sum(widened * widened), 'cell')]
    unnamed x7 -> x2, local copies, waits for them, and re-layouts: 17.2 us -> 0.01 us
    broadcast_in_dim x1 -> x2, local copies, waits for them, and re-layouts: 6.22 us -> 0.73 us  [the longest x1 0.65 us: solve(): relief = jnp.broadcast_to(relief[:, None], (tf_blocks, 8, width))]
  transfers between devices with their start and end apart: 3 -> 0, of which waited for: 3 -> 0; matrix products, arithmetic and copies ran while one was open for 11% -> 0% of each run, Pallas kernels for 0% -> 0%
where the time goes in v3:
time: 226 us; the launch traced here: 225 us
  Pallas kernels  218 us (96%)
  local copies, waits for them, and re-layouts  5 us (2%)
    pallas_call x1, Pallas kernels, solve(): pl.pallas_call(solve_kernel, out_shape=jax.ShapeDtypeStruct((cell_devices...  129 us
    pallas_call x1, Pallas kernels, activity_of(): pl.pallas_call(activity_kernel, out_shape=jax.ShapeDtypeStruct((devices,...  89.4 us

profile of v3, /device:TPU:1, one launch (start us, length us, event | category | flops | bytes accessed | tf_op | source)
XLA Modules:
  0.0 225.5 jit_solution(6106523120846818287)
XLA Ops:
  0.0 0.8 convert_bitcast_fusion
  0.8 0.1 broadcast_in_dim.20
  0.9 1.0 broadcast_in_dim.22.support_ref
  1.9 1.8 copy.14
  3.7 89.4 %activity.1.at_ref = bf16[16,112,1024]{2,1,0:T(8,128)(2,1)} custom-call(bf16[1024,1920]{1,0:T(8,128)(2,1)} %x_hbm.3, bf16[1920,1792]{1,0:T(8,128)(2,1)} %prior_hbm.1, bf16[7,15,16,256]{3,2,1,0:T(8,128)(2,1)} %broadcast_in_dim.22.support_ref, bf16[7,112,256]{2,1,0:T(8,128)(2,1)} %bitcast.21), custom_call_target="tpu_custom_call" | custom-call | tf_op jit(solution)/shard_map/activity/pallas_call | solution.py:185
  93.1 0.1 copy.8
  93.2 0.1 broadcast_in_dim.23
  93.3 0.7 broadcast_in_dim.25.relief_ref
  94.0 128.9 %solve.1 = bf16[8,224,256]{2,1,0:T(8,128)(2,1)} custom-call(bf16[16,112,1024]{2,1,0:T(8,128)(2,1)} %activity.1.at_ref, bf16[1024,1920]{1,0:T(8,128)(2,1)} %x_hbm.3, f32[14,8,256]{2,1,0:T(8,128)} %broadcast_in_dim.25.relief_ref), custom_call_target="tpu_custom_call" | custom-call | tf_op jit(solution)/shard_map/solve/pallas_call | solution.py:528
  222.9 1.3 copy.11
  224.1 1.3 slice_convert_fusion
  (5 shorter events, 0.1 us)

commit v4 on v3

v4 whole, which is shorter than its diff:
```python
import functools

import jax
import jax.numpy as jnp
from jax import lax
from jax.experimental import pallas as pl
from jax.experimental.pallas import tpu as pltpu
from jax.sharding import PartitionSpec as P

BLOCK = 128

OUT_UNITS = 100.0
LASSO = 0.006
RIDGE = 0.1
PRIOR_RELIEF = 0.7
EPSILON = 1e-06

MESH = pl.DeviceIdType.MESH
CHUNK = 256
SPLIT = 48
LAGS = (0, 1, 3, 5, 7, 9, 10)


class Spread:
    def __init__(self, ref, at, low, high, ys, across, partner, direct, handed):
        self.ref, (self.z, self.y, self.core) = ref, at
        self.rows = (low, high)
        self.ys, self.across, self.partner = ys, across, partner
        self.y_send, self.y_recv, self.z_send, self.z_recv, self.own_send, self.own_recv = direct
        self.fy_send, self.fy_recv, self.fz_send, self.fz_recv = handed

    def remote(self, block, send, recv, device):
        return pltpu.make_async_remote_copy(
            src_ref=block, dst_ref=block, send_sem=send, recv_sem=recv,
            device_id=device, device_id_type=MESH,
        )

    def own(self, side):
        block = self.ref.at[self.z, self.y, side]
        return self.remote(block, self.own_send, self.own_recv, self.partner)

    def over_y(self, k, device, y_to, slot):
        zs = slice(None) if k else self.z
        block = self.ref.at[zs, slot, self.core, self.rows[k]]
        return self.remote(block, self.y_send.at[k, y_to], self.y_recv.at[k, slot], device)

    def over_z(self, k, side):
        ys = self.y if k else slice(None)
        block = self.ref.at[side, ys, self.core, self.rows[k]]
        return self.remote(block, self.z_send.at[k], self.z_recv.at[k], self.across)

    def hand_y(self, k, slot, side):
        zs = slice(None) if k else self.z
        block = self.ref.at[zs, slot, side, self.rows[k]]
        return self.remote(block, self.fy_send.at[k, slot], self.fy_recv.at[k, slot], self.partner)

    def hand_z(self, k, side):
        ys = self.y if k else slice(None)
        block = self.ref.at[1 - self.z, ys, side, self.rows[k]]
        return self.remote(block, self.fz_send.at[k], self.fz_recv.at[k], self.partner)

    def begin(self):
        self.over_z(1, self.z).start()
        for y_to, device in self.ys:
            self.over_y(0, device, y_to, self.y).start()
        self.own(self.core).start()

    def relay_high(self):
        self.over_z(1, 1 - self.z).wait_recv()
        for y_to, device in self.ys:
            self.over_y(1, device, y_to, self.y).start()
        self.hand_z(1, self.core).start()

    def relay_low(self):
        for slot, device in self.ys:
            self.over_y(0, device, self.y, slot).wait_recv()
        self.over_z(0, self.z).start()
        for slot, _ in self.ys:
            self.hand_y(0, slot, self.core).start()

    def finish(self):
        for slot, device in self.ys:
            self.over_y(1, device, self.y, slot).wait_recv()
            self.hand_y(1, slot, self.core).start()
        self.over_z(0, 1 - self.z).wait_recv()
        self.hand_z(0, self.core).start()
        self.own(1 - self.core).wait_recv()
        for k in range(2):
            self.hand_z(k, 1 - self.core).wait_recv()
            for slot, _ in self.ys:
                self.hand_y(k, slot, 1 - self.core).wait_recv()

    def drain(self):
        self.own(self.core).wait_send()
        for k in range(2):
            self.over_z(k, self.z).wait_send()
            self.hand_z(k, self.core).wait_send()
            for y_to, device in self.ys:
                self.over_y(k, device, y_to, self.y).wait_send()
                self.hand_y(k, y_to, self.core).wait_send()


def activity_kernel(
    x_hbm, prior_hbm, mask_ref, gram_ref, at_ref,
    x, prior, support, part, pair, total, near_z, near_y, mid_z, mid_y, last_z, last_y, scores, acc,
    x_sem, prior_sem, pair_send, pair_recv,
    rs_y_send, rs_y_recv, rs_z_send, rs_z_recv,
    ag_y_send, ag_y_recv, ag_z_send, ag_z_recv, fw_send, fw_recv,
    at_y_send, at_y_recv, at_z_send, at_z_recv, own_send, own_recv,
    af_y_send, af_y_recv, af_z_send, af_z_recv,
):
    chunks, genes, _ = prior.shape
    me = lax.axis_index("gene")
    core, y, z = me % 2, (me // 2) % 4, me // 8
    partner = z * 8 + y * 2 + (1 - core)
    across = (1 - z) * 8 + y * 2 + core
    turns = (1, 3, 2)
    ys = [(y + dy) % 4 for dy in turns]

    x_copy = pltpu.make_async_copy(x_hbm, x, x_sem)

    def prior_copy(n):
        columns = pl.ds(pl.multiple_of(n * CHUNK, CHUNK), CHUNK)
        return pltpu.make_async_copy(prior_hbm.at[:, columns], prior.at[n], prior_sem.at[n])

    prior_copy(0).start()
    x_copy.start()
    for n in range(1, chunks):
        prior_copy(n).start()

    def device_of(y_to):
        return z * 8 + y_to * 2 + core

    barrier = pltpu.get_barrier_semaphore()
    for device in [device_of(y_to) for y_to in ys] + [across, partner]:
        pl.semaphore_signal(barrier, inc=1, device_id={"gene": device}, device_id_type=MESH)
    pl.semaphore_wait(barrier, len(ys) + 2)

    for b in range(mask_ref.shape[1]):
        lanes = slice(b % 2 * BLOCK, b % 2 * BLOCK + BLOCK)
        support[b // 2, :, lanes] = jnp.broadcast_to(
            mask_ref[:, b : b + 1].astype(jnp.float32), (support.shape[1], BLOCK)
        )

    def remote(src, dst, send, recv, device):
        return pltpu.make_async_remote_copy(
            src_ref=src, dst_ref=dst, send_sem=send, recv_sem=recv,
            device_id={"gene": device}, device_id_type=MESH,
        )

    def pair_copy(n):
        return remote(
            part.at[n, :, :, 1 - core], pair.at[n], pair_send.at[n], pair_recv.at[n], partner
        )

    def rs_y(n, z_first, y_to, slot):
        if z_first:
            src, dst = mid_z.at[n, y_to], last_z.at[n, slot]
        else:
            src, dst = total.at[n, :, y_to], near_y.at[n, slot]
        return remote(src, dst, rs_y_send.at[n, y_to], rs_y_recv.at[n, slot], device_of(y_to))

    def rs_z(n, z_first):
        if z_first:
            src, dst = total.at[n, 1 - z], near_z.at[n]
        else:
            src, dst = mid_y.at[n, 1 - z], last_y.at[n]
        return remote(src, dst, rs_z_send.at[n], rs_z_recv.at[n], across)

    def ag_y(n, z_first, y_to, slot):
        block = scores.at[n, :, slot, core] if z_first else scores.at[n, z, slot, core]
        return remote(
            block, block, ag_y_send.at[n, y_to], ag_y_recv.at[n, slot], device_of(y_to)
        )

    def ag_z(n, z_first, side):
        block = scores.at[n, side, y, core] if z_first else scores.at[n, side, :, core]
        return remote(block, block, ag_z_send.at[n], ag_z_recv.at[n], across)

    def fw_copy(n, side):
        block = scores.at[n, :, :, side]
        return remote(block, block, fw_send.at[n], fw_recv.at[n], partner)

    def wide(value):
        return value.astype(jnp.float32)

    def by_order(n, parity, step):
        @pl.when(n % 2 == parity)
        def _():
            step(True)

        @pl.when(n % 2 != parity)
        def _():
            step(False)

    def multiply(n):
        prior_copy(n).wait()

        rows = jnp.broadcast_to(support[n][:, None], (support.shape[1], 16, CHUNK))
        masked = prior[n].reshape(-1, BLOCK // 16, 16, CHUNK) * rows.astype(jnp.bfloat16)[:, None]
        prior[n] = masked.reshape(prior.shape[1:])
        product = jnp.dot(x[...], prior[n], preferred_element_type=jnp.float32)
        part[n] = product.astype(jnp.bfloat16).reshape(part.shape[1:])
        pair_copy(n).start()

    def spread(n):
        pair_copy(n).wait_recv()
        total[n] = (wide(part[n, :, :, core]) + wide(pair[n])).astype(jnp.bfloat16)

        def step(z_first):
            if z_first:
                rs_z(n, True).start()
            else:
                for y_to in ys:
                    rs_y(n, False, y_to, y).start()

        by_order(n, 0, step)

    def middle(n):
        def step(z_first):
            if z_first:
                rs_z(n, True).wait_recv()
                mid_z[n] = (wide(total[n, z]) + wide(near_z[n])).astype(jnp.bfloat16)
                for y_to in ys:
                    rs_y(n, True, y_to, y).start()
            else:
                value = wide(total[n, :, y])
                for slot in ys:
                    rs_y(n, False, y, slot).wait_recv()
                    value = value + wide(near_y[n, slot])
                mid_y[n] = value.astype(jnp.bfloat16)
                rs_z(n, False).start()

        by_order(n, 0, step)

    def collect(n):
        def step(z_first):
            if z_first:
                value = wide(mid_z[n, y])
                for slot in ys:
                    rs_y(n, True, y, slot).wait_recv()
                    value = value + wide(last_z[n, slot])
            else:
                rs_z(n, False).wait_recv()
                value = wide(mid_y[n, z]) + wide(last_y[n])
            scores[n, z, y, core] = value.astype(jnp.bfloat16)

        by_order(n, 0, step)

        def out(z_first):
            if z_first:
                ag_z(n, True, z).start()
            else:
                for y_to in ys:
                    ag_y(n, False, y_to, y).start()

        by_order(n, 1, out)

    def relay(n):
        def step(z_first):
            if z_first:
                ag_z(n, True, 1 - z).wait_recv()
                for y_to in ys:
                    ag_y(n, True, y_to, y).start()
            else:
                for slot in ys:
                    ag_y(n, False, y, slot).wait_recv()
                ag_z(n, False, z).start()

        by_order(n, 1, step)

    def share(n):
        def step(z_first):
            if z_first:
                for slot in ys:
                    ag_y(n, True, y, slot).wait_recv()
            else:
                ag_z(n, False, 1 - z).wait_recv()

        by_order(n, 1, step)
        fw_copy(n, core).start()

    acc[...] = jnp.zeros_like(acc)

    def mix(n):
        fw_copy(n, 1 - core).wait_recv()
        lanes = pl.ds(pl.multiple_of(n * CHUNK, CHUNK), CHUNK)
        acc[...] += lax.dot_general(
            gram_ref[:, lanes], scores[n].reshape(-1, CHUNK), (((1,), (1,)), ((), ())),
            preferred_element_type=jnp.float32,
        )

    x_copy.wait()
    stages = (
        (LAGS[0], multiply), (LAGS[1], spread), (LAGS[2], middle), (LAGS[3], collect),
        (LAGS[4], relay), (LAGS[5], share), (LAGS[6], mix),
    )

    def turn(i, carry):
        for lag, stage in stages:
            @pl.when((i >= lag) & (i < lag + chunks))
            def _():
                stage(i - lag)

        return carry

    lax.fori_loop(0, chunks + LAGS[-1], turn, 0)

    at_ref[z, y, core] = acc[...].astype(jnp.bfloat16)
    spread_at = Spread(
        at_ref, (z, y, core), slice(0, SPLIT), slice(SPLIT, at_ref.shape[3]),
        [(y_to, {"gene": device_of(y_to)}) for y_to in ys], {"gene": across}, {"gene": partner},
        (at_y_send, at_y_recv, at_z_send, at_z_recv, own_send, own_recv),
        (af_y_send, af_y_recv, af_z_send, af_z_recv),
    )
    spread_at.begin()
    spread_at.relay_high()
    spread_at.relay_low()
    spread_at.finish()

    def drain(n, carry):
        pair_copy(n).wait_send()
        fw_copy(n, core).wait_send()

        def reduced(z_first):
            rs_z(n, z_first).wait_send()
            for y_to in ys:
                rs_y(n, z_first, y_to, y).wait_send()

        by_order(n, 0, reduced)

        def gathered(z_first):
            ag_z(n, z_first, z).wait_send()
            for y_to in ys:
                ag_y(n, z_first, y_to, y).wait_send()

        by_order(n, 1, gathered)
        return carry

    lax.fori_loop(0, chunks, drain, 0)
    spread_at.drain()


def activity_of(expression, prior_values, block_mask, gram_inverse):
    devices = lax.axis_size("gene")
    cells, genes = expression.shape
    factors = prior_values.shape[1]
    own = gram_inverse.shape[1]
    chunks = factors // CHUNK
    rows = cells // devices
    bf = jnp.bfloat16
    vmem, dma = pltpu.VMEM, pltpu.SemaphoreType.DMA
    blocks = pl.pallas_call(
        activity_kernel,
        out_shape=jax.ShapeDtypeStruct((2, 4, 2, own, cells), bf),
        in_specs=[pl.BlockSpec(memory_space=pl.ANY)] * 2
        + [pl.BlockSpec(memory_space=pltpu.VMEM)] * 2,
        out_specs=pl.BlockSpec(memory_space=pltpu.VMEM),
        scratch_shapes=[
            vmem((cells, genes), bf),
            vmem((chunks, genes, CHUNK), bf),
            vmem((chunks, genes // BLOCK, CHUNK), jnp.float32),
            vmem((chunks, 2, 4, 2, rows, CHUNK), bf),
            vmem((chunks, 2, 4, rows, CHUNK), bf),
            vmem((chunks, 2, 4, rows, CHUNK), bf),
            vmem((chunks, 4, rows, CHUNK), bf),
            vmem((chunks, 4, 2, rows, CHUNK), bf),
            vmem((chunks, 4, rows, CHUNK), bf),
            vmem((chunks, 2, rows, CHUNK), bf),
            vmem((chunks, 4, rows, CHUNK), bf),
            vmem((chunks, rows, CHUNK), bf),
            vmem((chunks, 2, 4, 2, rows, CHUNK), bf),
            vmem((own, cells), jnp.float32),
            dma, dma((chunks,)), dma((chunks,)), dma((chunks,)),
            dma((chunks, 4)), dma((chunks, 4)), dma((chunks,)), dma((chunks,)),
            dma((chunks, 4)), dma((chunks, 4)), dma((chunks,)), dma((chunks,)),
            dma((chunks,)), dma((chunks,)),
            dma((2, 4)), dma((2, 4)), dma((2,)), dma((2,)), dma, dma,
            dma((2, 4)), dma((2, 4)), dma((2,)), dma((2,)),
        ],
        compiler_params=pltpu.CompilerParams(
            collective_id=0, has_side_effects=True, vmem_limit_bytes=56 * 2**20
        ),
        name="activity",
    )(expression, prior_values, block_mask, gram_inverse.T)
    return blocks


Z_ROWS = 1024
HOPS = 4
HELD = 5


def solve_kernel(
    at_ref, x_hbm, relief_ref, out_ref,
    x, part, z1, zs, x1, x2, xs, z2, gram_part, gram_z, gram_mid, gram_x, gram, squares, penalty,
    first, coef, coef_bf, sent,
    x_sem, z1_send, z1_recv, x1_send, x1_recv, x2_send, x2_recv, z2_send, z2_recv,
    gz_send, gz_recv, gx_send, gx_recv, hx_send, hx_recv, hz_send, hz_recv,
    gy_send, gy_recv, ga_send, ga_recv, own_send, own_recv, fy_send, fy_recv, fz_send, fz_recv,
    sq_send, sq_recv, out_send, out_recv,
):
    cells = 2 * HOPS
    pieces = at_ref.shape[3] // 16
    factors, width = first.shape
    cell, gene = lax.axis_index("cell"), lax.axis_index("gene")
    x_at, z_lo = cell % HOPS, cell // HOPS
    core, y_at, z_hi = gene % 2, (gene // 2) % 4, gene // 8
    z_partner = (1 - z_lo) * HOPS + x_at
    core_partner = z_hi * 8 + y_at * 2 + (1 - core)
    xs_at = [(x_at + dx) % HOPS for dx in (1, 3, 2)]
    ys_at = [(y_at + dy) % 4 for dy in (1, 3, 2)]
    across = (z_partner, (1 - z_hi) * 8 + y_at * 2 + core)

    def remote(src, dst, send, recv, at_cell, at_gene):
        return pltpu.make_async_remote_copy(
            src_ref=src, dst_ref=dst, send_sem=send, recv_sem=recv,
            device_id={"cell": at_cell, "gene": at_gene}, device_id_type=MESH,
        )

    tail = x_hbm.shape[1] - (cells - 1) * width

    def x_copy(d):
        lanes = tail if d == cells - 1 else width
        return pltpu.make_async_copy(
            x_hbm.at[:, pl.ds(d * width, lanes)], x.at[d, :, pl.ds(0, lanes)], x_sem.at[d]
        )

    for d in range(cells):
        x_copy(d).start()
    x[cells - 1, :, tail:] = jnp.zeros((x.shape[1], width - tail), x.dtype)

    barrier = pltpu.get_barrier_semaphore()
    greeted = [((cell + o) % cells, gene) for o in range(1, cells)]
    greeted += [(cell, z_hi * 8 + y_to * 2 + core) for y_to in ys_at]
    greeted += [across, (cell, core_partner)]
    for at_cell, at_gene in greeted:
        pl.semaphore_signal(
            barrier, inc=1, device_id={"cell": at_cell, "gene": at_gene}, device_id_type=MESH
        )
    pl.semaphore_wait(barrier, len(greeted))

    whole = at_ref[...].reshape(factors, -1)
    product = lax.dot_general(
        at_ref[z_hi, y_at, core], whole, (((1,), (1,)), ((), ())),
        preferred_element_type=jnp.float32,
    )
    gram_part[:pieces] = product.astype(jnp.bfloat16).reshape(pieces, 16, factors)
    gram_part[pieces:] = jnp.zeros_like(gram_part[pieces:])

    def gz_copy():
        src = gram_part.at[pl.ds((1 - z_lo) * HOPS, HOPS)]
        return remote(src, gram_z, gz_send, gz_recv, z_partner, gene)

    def gx_copy(x_to, slot):
        return remote(
            gram_mid.at[x_to], gram_x.at[slot], gx_send.at[x_to], gx_recv.at[slot],
            z_lo * HOPS + x_to, gene,
        )

    def hx_copy(x_to, slot):
        block = gram.at[z_hi, y_at, core, z_lo * HOPS + slot]
        return remote(
            block, block, hx_send.at[x_to], hx_recv.at[slot], z_lo * HOPS + x_to, gene
        )

    def hz_copy(side):
        block = gram.at[z_hi, y_at, core, pl.ds(side * HOPS, HOPS)]
        return remote(block, block, hz_send, hz_recv, z_partner, gene)

    gz_copy().start()

    for d in range(cells):
        x_copy(d).wait()

    def z1_copy(x_to):
        d = (1 - z_lo) * HOPS + x_to
        return remote(
            part.at[d, pl.ds(0, Z_ROWS)], z1.at[x_to], z1_send.at[x_to], z1_recv.at[x_to],
            z_partner, gene,
        )

    rest = pl.ds(Z_ROWS, factors - Z_ROWS)

    def x1_copy(z_to, x_to, slot):
        return remote(
            part.at[z_to * HOPS + x_to, rest], x1.at[slot, z_to],
            x1_send.at[x_to, z_to], x1_recv.at[slot, z_to], z_lo * HOPS + x_to, gene,
        )

    def x2_copy(x_to, slot):
        return remote(
            zs.at[x_to], x2.at[slot], x2_send.at[x_to], x2_recv.at[slot],
            z_lo * HOPS + x_to, gene,
        )

    def z2_copy():
        return remote(xs, z2, z2_send, z2_recv, z_partner, gene)

    def multiply(i, carry):
        x_to = (x_at + 1 + i) % HOPS
        z_to = (z_lo + 1 + i // HOPS) % 2
        d = z_to * HOPS + x_to
        value = jnp.dot(
            at_ref[...].reshape(factors, -1), x[d], preferred_element_type=jnp.float32
        )
        part[d] = value.astype(jnp.bfloat16)

        @pl.when(i < 2)
        def _():
            z1_copy(x_to).start()

        @pl.when((x_to != x_at) & (i != HELD))
        def _():
            x1_copy(z_to, x_to, x_at).start()

        return carry

    lax.fori_loop(0, HOPS, multiply, 0)

    gz_copy().wait_recv()
    mine = gram_part[pl.ds(z_lo * HOPS, HOPS)].astype(jnp.float32)
    gram_mid[...] = (mine + gram_z[...].astype(jnp.float32)).astype(jnp.bfloat16)
    for x_to in xs_at:
        gx_copy(x_to, x_at).start()

    lax.fori_loop(HOPS, cells, multiply, 0)

    def sq_copy(t, slot):
        return remote(squares.at[slot], squares.at[slot], sq_send.at[t], sq_recv.at[slot], t, gene)

    def square(b, total):
        value = at_ref[b // 8, b // 2 % 4, b % 2].astype(jnp.float32)
        return total + jnp.sum((value * value).reshape(-1, 8, value.shape[1]), axis=0)

    squares[cell] = lax.fori_loop(
        0, 16, square, jnp.zeros(squares.shape[1:], jnp.float32)
    )
    for o in range(1, cells):
        sq_copy((cell + o) % cells, cell).start()

    for b in range(relief_ref.shape[0]):
        rows = jnp.broadcast_to(relief_ref[b][None], (BLOCK // 8, 8, width))
        penalty[pl.ds(b * BLOCK, BLOCK)] = rows.reshape(BLOCK, width)

    def pair_sum(i):
        x_to = (x_at + 1 + i) % HOPS
        z1_copy(x_to).wait_recv()
        own = part[z_lo * HOPS + x_to, :Z_ROWS].astype(jnp.float32)
        zs[x_to] = (own + z1[x_to].astype(jnp.float32)).astype(jnp.bfloat16)
        if i < HOPS - 1:
            x2_copy(x_to, x_at).start()

    value = gram_mid[x_at].astype(jnp.float32)
    for slot in xs_at:
        gx_copy(x_at, slot).wait_recv()
        value = value + gram_x[slot].astype(jnp.float32)
    gram[z_hi, y_at, core, cell] = value.astype(jnp.bfloat16)
    for x_to in xs_at:
        hx_copy(x_to, x_at).start()
    x1_copy(z_lo, (x_at + 1 + HELD) % HOPS, x_at).start()

    pair_sum(0)

    for slot in xs_at:
        hx_copy(x_at, slot).wait_recv()
    hz_copy(z_lo).start()
    for i in range(2, HOPS):
        z1_copy((x_at + 1 + i) % HOPS).start()

    pair_sum(1)

    hz_copy(1 - z_lo).wait_recv()
    spread = Spread(
        gram, (z_hi, y_at, core), slice(0, HOPS), slice(HOPS, pieces),
        [(y_to, {"cell": cell, "gene": z_hi * 8 + y_to * 2 + core}) for y_to in ys_at],
        {"cell": across[0], "gene": across[1]}, {"cell": cell, "gene": core_partner},
        (gy_send, gy_recv, ga_send, ga_recv, own_send, own_recv),
        (fy_send, fy_recv, fz_send, fz_recv),
    )
    spread.begin()
    spread.relay_high()
    pair_sum(2)
    spread.relay_low()

    value = part[(1 - z_lo) * HOPS + x_at, Z_ROWS:].astype(jnp.float32)
    for o in range(1, HOPS):
        slot = (x_at + o) % HOPS
        x1_copy(1 - z_lo, x_at, slot).wait_recv()
        value = value + x1[slot, 1 - z_lo].astype(jnp.float32)
    xs[...] = value.astype(jnp.bfloat16)
    z2_copy().start()

    pair_sum(3)

    for o in range(1, cells):
        sq_copy(cell, (cell + o) % cells).wait_recv()
    sum_squares = jnp.sum(jnp.sum(squares[...], axis=0), keepdims=True)
    total_cells = cells * x.shape[1]
    step_size = 0.5 / (sum_squares / (total_cells * factors) + EPSILON)
    scale = step_size / total_cells
    inverse = 1.0 / (1.0 + step_size * RIDGE)

    def shrunk(moved, rows):
        limit = step_size * penalty[rows]
        return (jnp.maximum(moved - limit, 0.0) - jnp.maximum(-moved - limit, 0.0)) * inverse

    def start_from(value, rows):
        first[rows] = value
        start = shrunk(scale * value, rows)
        coef[rows] = start
        coef_bf[rows] = start.astype(jnp.bfloat16)

    for o in range(1, HOPS):
        slot = (x_at + o) % HOPS
        x2_copy(x_at, slot).wait_recv()
        x1_copy(z_lo, x_at, slot).wait_recv()

    def z_block(b, carry):
        rows = pl.ds(pl.multiple_of(b * BLOCK, BLOCK), BLOCK)
        value = zs[x_at, rows].astype(jnp.float32)
        for o in range(1, HOPS):
            value = value + x2[(x_at + o) % HOPS, rows].astype(jnp.float32)
        start_from(value, rows)
        return carry

    lax.fori_loop(0, Z_ROWS // BLOCK, z_block, 0)
    z2_copy().wait_recv()

    def x_block(b, carry):
        low = pl.ds(pl.multiple_of(b * BLOCK, BLOCK), BLOCK)
        rows = pl.ds(pl.multiple_of(b * BLOCK + Z_ROWS, BLOCK), BLOCK)
        value = part[cell, rows].astype(jnp.float32) + z2[low].astype(jnp.float32)
        for o in range(1, HOPS):
            value = value + x1[(x_at + o) % HOPS, z_lo, low].astype(jnp.float32)
        start_from(value, rows)
        return carry

    lax.fori_loop(0, (factors - Z_ROWS) // BLOCK, x_block, 0)

    spread.finish()
    height = out_ref.shape[1]

    def out_copy(t, slot):
        return remote(sent.at[t], out_ref.at[slot], out_send.at[t], out_recv.at[slot], t, gene)

    def finish(i, carry):
        t = (cell + 1 + i) % cells
        rows = pl.ds(pl.multiple_of(t * height, 32), height)
        block = gram[t // 4, t % 4, :, :pieces].reshape(height, factors)
        second = jnp.dot(block, coef_bf[...], preferred_element_type=jnp.float32)
        moved = coef[rows] - scale * (second - first[rows])
        value = (shrunk(moved, rows) * OUT_UNITS).astype(jnp.bfloat16)

        @pl.when(i < cells - 1)
        def _():
            sent[t] = value
            out_copy(t, cell).start()

        @pl.when(i == cells - 1)
        def _():
            out_ref[cell] = value

        return carry

    lax.fori_loop(0, cells, finish, 0)

    gz_copy().wait_send()
    hz_copy(z_lo).wait_send()
    for x_to in xs_at:
        gx_copy(x_to, x_at).wait_send()
        hx_copy(x_to, x_at).wait_send()
    spread.drain()

    for x_to in range(HOPS):
        z1_copy(x_to).wait_send()
    for o in range(1, HOPS):
        x_to = (x_at + o) % HOPS
        x2_copy(x_to, x_at).wait_send()
        for z_to in range(2):
            x1_copy(z_to, x_to, x_at).wait_send()
    z2_copy().wait_send()
    for o in range(1, cells):
        t = (cell + o) % cells
        sq_copy(t, cell).wait_send()
        out_copy(t, cell).wait_send()
        out_copy(cell, t).wait_recv()


def solve(activity_t, expression, block_mask):
    cell_devices, gene_devices = lax.axis_size("cell"), lax.axis_size("gene")
    own, cells = activity_t.shape[-2:]
    factors = gene_devices * own
    width = CHUNK
    gene_blocks, tf_blocks = block_mask.shape
    per = width // BLOCK
    relief = jnp.pad(block_mask.T.astype(jnp.float32), ((0, 0), (0, cell_devices * per - gene_blocks)))
    relief = lax.dynamic_slice_in_dim(relief, lax.axis_index("cell") * per, per, 1)
    relief = jnp.repeat(LASSO * (1.0 - PRIOR_RELIEF * relief), BLOCK, axis=1)
    relief = jnp.broadcast_to(relief[:, None], (tf_blocks, 8, width))
    rest = factors - Z_ROWS
    bf, f32 = jnp.bfloat16, jnp.float32
    vmem, dma = pltpu.VMEM, pltpu.SemaphoreType.DMA
    return pl.pallas_call(
        solve_kernel,
        out_shape=jax.ShapeDtypeStruct((cell_devices, factors // cell_devices, width), bf),
        in_specs=[
            pl.BlockSpec(memory_space=pltpu.VMEM),
            pl.BlockSpec(memory_space=pl.ANY),
            pl.BlockSpec(memory_space=pltpu.VMEM),
        ],
        out_specs=pl.BlockSpec(memory_space=pltpu.VMEM),
        scratch_shapes=[
            vmem((cell_devices, cells, width), bf),
            vmem((cell_devices, factors, width), bf),
            vmem((HOPS, Z_ROWS, width), bf),
            vmem((HOPS, Z_ROWS, width), bf),
            vmem((HOPS, 2, rest, width), bf),
            vmem((HOPS, Z_ROWS, width), bf),
            vmem((rest, width), bf),
            vmem((rest, width), bf),
            vmem((cell_devices, 16, factors), bf),
            vmem((HOPS, 16, factors), bf),
            vmem((HOPS, 16, factors), bf),
            vmem((HOPS, 16, factors), bf),
            vmem((2, 4, 2, cell_devices, 16, factors), bf),
            vmem((cell_devices, 8, cells), f32),
            vmem((factors, width), f32),
            vmem((factors, width), f32),
            vmem((factors, width), f32),
            vmem((factors, width), bf),
            vmem((cell_devices, factors // cell_devices, width), bf),
            dma((cell_devices,)),
            dma((HOPS,)), dma((HOPS,)),
            dma((HOPS, 2)), dma((HOPS, 2)),
            dma((HOPS,)), dma((HOPS,)),
            dma, dma,
            dma, dma, dma((HOPS,)), dma((HOPS,)), dma((HOPS,)), dma((HOPS,)), dma, dma,
            dma((2, 4)), dma((2, 4)), dma((2,)), dma((2,)), dma, dma,
            dma((2, 4)), dma((2, 4)), dma((2,)), dma((2,)),
            dma((cell_devices,)), dma((cell_devices,)),
            dma((cell_devices,)), dma((cell_devices,)),
        ],
        compiler_params=pltpu.CompilerParams(
            collective_id=1, has_side_effects=True, vmem_limit_bytes=60 * 2**20
        ),
        name="solve",
    )(activity_t, expression, relief)


def on_device(expression, prior_values, block_mask, gram_inverse):
    activity_t = activity_of(expression, prior_values, block_mask, gram_inverse)
    blocks = solve(activity_t, expression, block_mask)
    rows = blocks.shape[1]
    whole = blocks.transpose(1, 0, 2).reshape(rows, -1)
    return whole[:, : expression.shape[1]].astype(jnp.float32)


def solution(mesh):
    in_specs = (P("cell", "gene"), P("gene", None), P("gene", None), P(None, "gene"))
    out_specs = P("cell", "gene")
    return jax.shard_map(
        on_device, mesh=mesh, in_specs=in_specs, out_specs=out_specs, check_vma=False
    )
```

time: 226 us -> 180 us (0.80)
  Pallas kernels: 218 us -> 176 us
  local copies, waits for them, and re-layouts: 5 us -> 2.12 us
    pallas_call x1, Pallas kernels: 129 us -> 100 us  [solve(): pl.pallas_call(solve_kernel, out_shape=jax.ShapeDtypeStruct((cell_devices...]
    pallas_call x1, Pallas kernels: 89.4 us -> 75.4 us  [activity_of(): pl.pallas_call(activity_kernel, out_shape=jax.ShapeDtypeStruct((2, 4, 2,...]
where the time goes in v4:
time: 180 us
  Pallas kernels  176 us (98%)
  local copies, waits for them, and re-layouts  2.12 us (1%)
  other arithmetic  2.03 us (1%)
    pallas_call x1, Pallas kernels, solve(): pl.pallas_call(solve_kernel, out_shape=jax.ShapeDtypeStruct((cell_devices...  100 us
    pallas_call x1, Pallas kernels, activity_of(): pl.pallas_call(activity_kernel, out_shape=jax.ShapeDtypeStruct((2, 4, 2,...  75.4 us

profile of v4, /device:TPU:1, one launch (start us, length us, event | category | flops | bytes accessed | tf_op | source)
XLA Modules:
  0.0 179.9 jit_solution(8754031334371463884)
XLA Ops:
  0.0 0.7 convert_bitcast_fusion
  0.7 0.1 copy.6
  0.8 0.1 broadcast_in_dim.10
  0.9 0.7 broadcast_in_dim.12.relief_ref
  1.6 75.4 %activity.1.at_ref = bf16[2,4,2,112,1024]{4,3,2,1,0:T(8,128)(2,1)} custom-call(bf16[1024,1920]{1,0:T(8,128)(2,1)} %x_hbm.3, bf16[1920,1792]{1,0:T(8,128)(2,1)} %prior_hbm.1, s32[15,14]{1,0:T(8,128)} %mask_ref.1, bf16[112,1792]{1,0:T(8,128)(2,1)} %bitcast.11), custom_call_target="tpu_custom_call" | custom-call | tf_op jit(solution)/shard_map/activity/pallas_call | solution.py:353
  77.0 100.3 %solve.1 = bf16[8,224,256]{2,1,0:T(8,128)(2,1)} custom-call(bf16[2,4,2,112,1024]{4,3,2,1,0:T(8,128)(2,1)} %activity.1.at_ref, bf16[1024,1920]{1,0:T(8,128)(2,1)} %x_hbm.3, f32[14,8,256]{2,1,0:T(8,128)} %broadcast_in_dim.12.relief_ref), custom_call_target="tpu_custom_call" | custom-call | tf_op jit(solution)/shard_map/solve/pallas_call | solution.py:704
  177.3 1.3 copy.8
  178.6 1.3 slice_convert_fusion
  (3 shorter events, 0.0 us)

commit v5 on v4

--- a/solution.py
+++ b/solution.py
@@ -18,7 +18,7 @@
 MESH = pl.DeviceIdType.MESH
 CHUNK = 256
 SPLIT = 48
-LAGS = (0, 1, 3, 5, 7, 9, 10)
+LAGS = (0, 1, 4, 7, 11, 15, 16)
 
 
 class Spread:
@@ -386,16 +386,16 @@
     return blocks
 
 
-Z_ROWS = 1024
+Z_ROWS = 768
 HOPS = 4
-HELD = 5
 
 
 def solve_kernel(
     at_ref, x_hbm, relief_ref, out_ref,
-    x, part, z1, zs, x1, x2, xs, z2, gram_part, gram_z, gram_mid, gram_x, gram, squares, penalty,
+    x, part, z1, zs, r1, x1, r2, x2, xs, z2, gram_part, gram_z, gram_mid, gram_x, gram, squares, penalty,
     first, coef, coef_bf, sent,
-    x_sem, z1_send, z1_recv, x1_send, x1_recv, x2_send, x2_recv, z2_send, z2_recv,
+    x_sem, z1_send, z1_recv, r1_send, r1_recv, x1_send, x1_recv, r2_send, r2_recv,
+    x2_send, x2_recv, z2_send, z2_recv,
     gz_send, gz_recv, gx_send, gx_recv, hx_send, hx_recv, hz_send, hz_recv,
     gy_send, gy_recv, ga_send, ga_recv, own_send, own_recv, fy_send, fy_recv, fz_send, fz_recv,
     sq_send, sq_recv, out_send, out_recv,
@@ -408,7 +408,8 @@
     core, y_at, z_hi = gene % 2, (gene // 2) % 4, gene // 8
     z_partner = (1 - z_lo) * HOPS + x_at
     core_partner = z_hi * 8 + y_at * 2 + (1 - core)
-    xs_at = [(x_at + dx) % HOPS for dx in (1, 3, 2)]
+    right, left, far = [(x_at + dx) % HOPS for dx in (1, 3, 2)]
+    xs_at = [right, left, far]
     ys_at = [(y_at + dy) % 4 for dy in (1, 3, 2)]
     across = (z_partner, (1 - z_hi) * 8 + y_at * 2 + core)
 
@@ -482,23 +483,51 @@
 
     rest = pl.ds(Z_ROWS, factors - Z_ROWS)
 
-    def x1_copy(z_to, x_to, slot):
+    def toward(k):
+        return z_lo * HOPS + (left if k else right)
+
+    def r1_copy(k):
+        z_to = z_lo if k else 1 - z_lo
         return remote(
-            part.at[z_to * HOPS + x_to, rest], x1.at[slot, z_to],
-            x1_send.at[x_to, z_to], x1_recv.at[slot, z_to], z_lo * HOPS + x_to, gene,
-        )
-
-    def x2_copy(x_to, slot):
+            part.at[z_to * HOPS + far, rest], r1.at[k], r1_send.at[k], r1_recv.at[k],
+            toward(k), gene,
+        )
+
+    def x1_copy(z_to, k):
         return remote(
-            zs.at[x_to], x2.at[slot], x2_send.at[x_to], x2_recv.at[slot],
-            z_lo * HOPS + x_to, gene,
+            part.at[z_to * HOPS + (left if k else right), rest], x1.at[z_to, k],
+            x1_send.at[z_to, k], x1_recv.at[z_to, k], toward(k), gene,
+        )
+
+    def pass_on(k):
+        z_to = z_lo if k else 1 - z_lo
+        d = z_to * HOPS + (left if k else right)
+        r1_copy(k).wait_recv()
+        value = part[d, Z_ROWS:].astype(jnp.float32) + r1[k].astype(jnp.float32)
+        part[d, Z_ROWS:] = value.astype(jnp.bfloat16)
+        x1_copy(z_to, k).start()
+
+    half = Z_ROWS // 2
+
+    def r2_copy(k):
+        return remote(
+            zs.at[far, pl.ds(k * half, half)], r2.at[k], r2_send.at[k], r2_recv.at[k],
+            toward(k), gene,
+        )
+
+    def x2_copy(k):
+        return remote(
+            zs.at[left if k else right], x2.at[k], x2_send.at[k], x2_recv.at[k], toward(k), gene
         )
 
     def z2_copy():
         return remote(xs, z2, z2_send, z2_recv, z_partner, gene)
 
+    def order(i):
+        return (x_at + 2 - i + (i // 2) * (2 * i - 1)) % HOPS
+
     def multiply(i, carry):
-        x_to = (x_at + 1 + i) % HOPS
+        x_to = order(i % HOPS)
         z_to = (z_lo + 1 + i // HOPS) % 2
         d = z_to * HOPS + x_to
         value = jnp.dot(
@@ -510,9 +539,13 @@
         def _():
             z1_copy(x_to).start()
 
-        @pl.when((x_to != x_at) & (i != HELD))
+        @pl.when(i == 0)
         def _():
-            x1_copy(z_to, x_to, x_at).start()
+            r1_copy(0).start()
+
+        @pl.when(i == 2)
+        def _():
+            x1_copy(1 - z_lo, 1).start()
 
         return carry
 
@@ -544,12 +577,21 @@
         penalty[pl.ds(b * BLOCK, BLOCK)] = rows.reshape(BLOCK, width)
 
     def pair_sum(i):
-        x_to = (x_at + 1 + i) % HOPS
+        x_to = order(i)
         z1_copy(x_to).wait_recv()
         own = part[z_lo * HOPS + x_to, :Z_ROWS].astype(jnp.float32)
-        zs[x_to] = (own + z1[x_to].astype(jnp.float32)).astype(jnp.bfloat16)
-        if i < HOPS - 1:
-            x2_copy(x_to, x_at).start()
+        value = own + z1[x_to].astype(jnp.float32)
+        zs[x_to] = value.astype(jnp.bfloat16)
+        if i == 0:
+            r2_copy(0).start()
+            r2_copy(1).start()
+        elif i < HOPS - 1:
+            k = i - 1
+            rows = pl.ds(k * half, half)
+            r2_copy(k).wait_recv()
+            value = zs[x_to, rows].astype(jnp.float32) + r2[k].astype(jnp.float32)
+            zs[x_to, rows] = value.astype(jnp.bfloat16)
+            x2_copy(k).start()
 
     value = gram_mid[x_at].astype(jnp.float32)
     for slot in xs_at:
@@ -558,17 +600,16 @@
     gram[z_hi, y_at, core, cell] = value.astype(jnp.bfloat16)
     for x_to in xs_at:
         hx_copy(x_to, x_at).start()
-    x1_copy(z_lo, (x_at + 1 + HELD) % HOPS, x_at).start()
-
+    r1_copy(1).start()
+    pass_on(0)
     pair_sum(0)
+    x1_copy(z_lo, 0).start()
 
     for slot in xs_at:
         hx_copy(x_at, slot).wait_recv()
     hz_copy(z_lo).start()
     for i in range(2, HOPS):
-        z1_copy((x_at + 1 + i) % HOPS).start()
-
-    pair_sum(1)
+        z1_copy(order(i)).start()
 
     hz_copy(1 - z_lo).wait_recv()
     spread = Spread(
@@ -579,18 +620,18 @@
         (fy_send, fy_recv, fz_send, fz_recv),
     )
     spread.begin()
+    pass_on(1)
     spread.relay_high()
+    pair_sum(1)
     pair_sum(2)
-    spread.relay_low()
 
     value = part[(1 - z_lo) * HOPS + x_at, Z_ROWS:].astype(jnp.float32)
-    for o in range(1, HOPS):
-        slot = (x_at + o) % HOPS
-        x1_copy(1 - z_lo, x_at, slot).wait_recv()
-        value = value + x1[slot, 1 - z_lo].astype(jnp.float32)
+    for k in range(2):
+        x1_copy(1 - z_lo, k).wait_recv()
+        value = value + x1[1 - z_lo, k].astype(jnp.float32)
     xs[...] = value.astype(jnp.bfloat16)
     z2_copy().start()
-
+    spread.relay_low()
     pair_sum(3)
 
     for o in range(1, cells):
@@ -611,16 +652,15 @@
         coef[rows] = start
         coef_bf[rows] = start.astype(jnp.bfloat16)
 
-    for o in range(1, HOPS):
-        slot = (x_at + o) % HOPS
-        x2_copy(x_at, slot).wait_recv()
-        x1_copy(z_lo, x_at, slot).wait_recv()
+    for k in range(2):
+        x2_copy(k).wait_recv()
+        x1_copy(z_lo, k).wait_recv()
 
     def z_block(b, carry):
         rows = pl.ds(pl.multiple_of(b * BLOCK, BLOCK), BLOCK)
         value = zs[x_at, rows].astype(jnp.float32)
-        for o in range(1, HOPS):
-            value = value + x2[(x_at + o) % HOPS, rows].astype(jnp.float32)
+        for k in range(2):
+            value = value + x2[k, rows].astype(jnp.float32)
         start_from(value, rows)
         return carry
 
@@ -631,8 +671,8 @@
         low = pl.ds(pl.multiple_of(b * BLOCK, BLOCK), BLOCK)
         rows = pl.ds(pl.multiple_of(b * BLOCK + Z_ROWS, BLOCK), BLOCK)
         value = part[cell, rows].astype(jnp.float32) + z2[low].astype(jnp.float32)
-        for o in range(1, HOPS):
-            value = value + x1[(x_at + o) % HOPS, z_lo, low].astype(jnp.float32)
+        for k in range(2):
+            value = value + x1[z_lo, k, low].astype(jnp.float32)
         start_from(value, rows)
         return carry
 
@@ -645,25 +685,28 @@
         return remote(sent.at[t], out_ref.at[slot], out_send.at[t], out_recv.at[slot], t, gene)
 
     def finish(i, carry):
-        t = (cell + 1 + i) % cells
-        rows = pl.ds(pl.multiple_of(t * height, 32), height)
-        block = gram[t // 4, t % 4, :, :pieces].reshape(height, factors)
+        p = (cell // 2 + 1 + i) % HOPS
+        rows = pl.ds(pl.multiple_of(p * (2 * height), 64), 2 * height)
+        block = gram[p // 2, pl.ds(p % 2 * 2, 2), :, :pieces].reshape(2 * height, factors)
         second = jnp.dot(block, coef_bf[...], preferred_element_type=jnp.float32)
         moved = coef[rows] - scale * (second - first[rows])
         value = (shrunk(moved, rows) * OUT_UNITS).astype(jnp.bfloat16)
-
-        @pl.when(i < cells - 1)
-        def _():
-            sent[t] = value
-            out_copy(t, cell).start()
-
-        @pl.when(i == cells - 1)
-        def _():
-            out_ref[cell] = value
+        for h in range(2):
+            t = 2 * p + h
+            piece = value[h * height : (h + 1) * height]
+
+            @pl.when(t != cell)
+            def _():
+                sent[t] = piece
+                out_copy(t, cell).start()
+
+            @pl.when(t == cell)
+            def _():
+                out_ref[cell] = piece
 
         return carry
 
-    lax.fori_loop(0, cells, finish, 0)
+    lax.fori_loop(0, HOPS, finish, 0)
 
     gz_copy().wait_send()
     hz_copy(z_lo).wait_send()
@@ -674,11 +717,12 @@
 
     for x_to in range(HOPS):
         z1_copy(x_to).wait_send()
-    for o in range(1, HOPS):
-        x_to = (x_at + o) % HOPS
-        x2_copy(x_to, x_at).wait_send()
+    for k in range(2):
+        r1_copy(k).wait_send()
+        r2_copy(k).wait_send()
+        x2_copy(k).wait_send()
         for z_to in range(2):
-            x1_copy(z_to, x_to, x_at).wait_send()
+            x1_copy(z_to, k).wait_send()
     z2_copy().wait_send()
     for o in range(1, cells):
         t = (cell + o) % cells
@@ -715,8 +759,10 @@
             vmem((cell_devices, factors, width), bf),
             vmem((HOPS, Z_ROWS, width), bf),
             vmem((HOPS, Z_ROWS, width), bf),
-            vmem((HOPS, 2, rest, width), bf),
-            vmem((HOPS, Z_ROWS, width), bf),
+            vmem((2, rest, width), bf),
+            vmem((2, 2, rest, width), bf),
+            vmem((2, Z_ROWS // 2, width), bf),
+            vmem((2, Z_ROWS, width), bf),
             vmem((rest, width), bf),
             vmem((rest, width), bf),
             vmem((cell_devices, 16, factors), bf),
@@ -732,8 +778,8 @@
             vmem((cell_devices, factors // cell_devices, width), bf),
             dma((cell_devices,)),
             dma((HOPS,)), dma((HOPS,)),
-            dma((HOPS, 2)), dma((HOPS, 2)),
-            dma((HOPS,)), dma((HOPS,)),
+            dma((2,)), dma((2,)), dma((2, 2)), dma((2, 2)),
+            dma((2,)), dma((2,)), dma((2,)), dma((2,)),
             dma, dma,
             dma, dma, dma((HOPS,)), dma((HOPS,)), dma((HOPS,)), dma((HOPS,)), dma, dma,
             dma((2, 4)), dma((2, 4)), dma((2,)), dma((2,)), dma, dma,

time: 180 us -> 163 us (0.906)
  Pallas kernels: 176 us -> 158 us
    pallas_call x1, Pallas kernels: 100 us -> 86.6 us  [solve(): pl.pallas_call(solve_kernel, out_shape=jax.ShapeDtypeStruct((cell_devices...]
    pallas_call x1, Pallas kernels: 75.4 us -> 71.5 us  [activity_of(): pl.pallas_call(activity_kernel, out_shape=jax.ShapeDtypeStruct((2, 4, 2,...]
where the time goes in v5:
time: 163 us; the launch traced here: 162 us
  Pallas kernels  158 us (97%)
  local copies, waits for them, and re-layouts  2.12 us (1%)
  other arithmetic  2.03 us (1%)
    pallas_call x1, Pallas kernels, solve(): pl.pallas_call(solve_kernel, out_shape=jax.ShapeDtypeStruct((cell_devices...  86.6 us
    pallas_call x1, Pallas kernels, activity_of(): pl.pallas_call(activity_kernel, out_shape=jax.ShapeDtypeStruct((2, 4, 2,...  71.5 us

profile of v5, /device:TPU:1, one launch (start us, length us, event | category | flops | bytes accessed | tf_op | source)
XLA Modules:
  0.0 162.3 jit_solution(3012341996471931415)
XLA Ops:
  0.0 0.7 convert_bitcast_fusion
  0.7 0.1 copy.6
  0.8 0.1 broadcast_in_dim.10
  0.9 0.7 broadcast_in_dim.12.relief_ref
  1.6 71.5 %activity.1.at_ref = bf16[2,4,2,112,1024]{4,3,2,1,0:T(8,128)(2,1)} custom-call(bf16[1024,1920]{1,0:T(8,128)(2,1)} %x_hbm.3, bf16[1920,1792]{1,0:T(8,128)(2,1)} %prior_hbm.1, s32[15,14]{1,0:T(8,128)} %mask_ref.1, bf16[112,1792]{1,0:T(8,128)(2,1)} %bitcast.11), custom_call_target="tpu_custom_call" | custom-call | tf_op jit(solution)/shard_map/activity/pallas_call | solution.py:353
  73.1 86.6 %solve.1 = bf16[8,224,256]{2,1,0:T(8,128)(2,1)} custom-call(bf16[2,4,2,112,1024]{4,3,2,1,0:T(8,128)(2,1)} %activity.1.at_ref, bf16[1024,1920]{1,0:T(8,128)(2,1)} %x_hbm.3, f32[14,8,256]{2,1,0:T(8,128)} %broadcast_in_dim.12.relief_ref), custom_call_target="tpu_custom_call" | custom-call | tf_op jit(solution)/shard_map/solve/pallas_call | solution.py:748
  159.7 1.3 copy.8
  161.0 1.3 slice_convert_fusion
  (3 shorter events, 0.0 us)

commit v6 on v5

--- a/solution.py
+++ b/solution.py
@@ -391,10 +391,10 @@
 
 
 def solve_kernel(
-    at_ref, x_hbm, relief_ref, out_ref,
-    x, part, z1, zs, r1, x1, r2, x2, xs, z2, gram_part, gram_z, gram_mid, gram_x, gram, squares, penalty,
+    at_hbm, x_hbm, mask_ref, out_ref,
+    at_ref, x, part, z1, zs, r1, x1, r2, x2, xs, z2, gram_part, gram_z, gram_mid, gram_x, gram, squares, penalty,
     first, coef, coef_bf, sent,
-    x_sem, z1_send, z1_recv, r1_send, r1_recv, x1_send, x1_recv, r2_send, r2_recv,
+    at_sem, x_sem, z1_send, z1_recv, r1_send, r1_recv, x1_send, x1_recv, r2_send, r2_recv,
     x2_send, x2_recv, z2_send, z2_recv,
     gz_send, gz_recv, gx_send, gx_recv, hx_send, hx_recv, hz_send, hz_recv,
     gy_send, gy_recv, ga_send, ga_recv, own_send, own_recv, fy_send, fy_recv, fz_send, fz_recv,
@@ -427,6 +427,8 @@
             x_hbm.at[:, pl.ds(d * width, lanes)], x.at[d, :, pl.ds(0, lanes)], x_sem.at[d]
         )
 
+    at_copy = pltpu.make_async_copy(at_hbm, at_ref, at_sem)
+    at_copy.start()
     for d in range(cells):
         x_copy(d).start()
     x[cells - 1, :, tail:] = jnp.zeros((x.shape[1], width - tail), x.dtype)
@@ -441,6 +443,7 @@
         )
     pl.semaphore_wait(barrier, len(greeted))
 
+    at_copy.wait()
     whole = at_ref[...].reshape(factors, -1)
     product = lax.dot_general(
         at_ref[z_hi, y_at, core], whole, (((1,), (1,)), ((), ())),
@@ -572,9 +575,13 @@
     for o in range(1, cells):
         sq_copy((cell + o) % cells, cell).start()
 
-    for b in range(relief_ref.shape[0]):
-        rows = jnp.broadcast_to(relief_ref[b][None], (BLOCK // 8, 8, width))
-        penalty[pl.ds(b * BLOCK, BLOCK)] = rows.reshape(BLOCK, width)
+    for h in range(width // BLOCK):
+        gene_block = 2 * cell + h * (1 - cell // (cells - 1))
+        relief = mask_ref[pl.ds(gene_block, 1)].astype(jnp.float32)
+        row = LASSO * (1.0 - PRIOR_RELIEF * relief)
+        for b in range(mask_ref.shape[1]):
+            block = jnp.broadcast_to(row[:, b : b + 1], (BLOCK, BLOCK))
+            penalty[b * BLOCK : (b + 1) * BLOCK, h * BLOCK : (h + 1) * BLOCK] = block
 
     def pair_sum(i):
         x_to = order(i)
@@ -679,10 +686,11 @@
     lax.fori_loop(0, (factors - Z_ROWS) // BLOCK, x_block, 0)
 
     spread.finish()
-    height = out_ref.shape[1]
+    height = out_ref.shape[0]
 
     def out_copy(t, slot):
-        return remote(sent.at[t], out_ref.at[slot], out_send.at[t], out_recv.at[slot], t, gene)
+        lanes = pl.ds(pl.multiple_of(slot * width, width), width)
+        return remote(sent.at[t], out_ref.at[:, lanes], out_send.at[t], out_recv.at[slot], t, gene)
 
     def finish(i, carry):
         p = (cell // 2 + 1 + i) % HOPS
@@ -702,7 +710,7 @@
 
             @pl.when(t == cell)
             def _():
-                out_ref[cell] = piece
+                out_ref[:, pl.ds(pl.multiple_of(cell * width, width), width)] = piece
 
         return carry
 
@@ -736,25 +744,20 @@
     own, cells = activity_t.shape[-2:]
     factors = gene_devices * own
     width = CHUNK
-    gene_blocks, tf_blocks = block_mask.shape
-    per = width // BLOCK
-    relief = jnp.pad(block_mask.T.astype(jnp.float32), ((0, 0), (0, cell_devices * per - gene_blocks)))
-    relief = lax.dynamic_slice_in_dim(relief, lax.axis_index("cell") * per, per, 1)
-    relief = jnp.repeat(LASSO * (1.0 - PRIOR_RELIEF * relief), BLOCK, axis=1)
-    relief = jnp.broadcast_to(relief[:, None], (tf_blocks, 8, width))
     rest = factors - Z_ROWS
     bf, f32 = jnp.bfloat16, jnp.float32
     vmem, dma = pltpu.VMEM, pltpu.SemaphoreType.DMA
     return pl.pallas_call(
         solve_kernel,
-        out_shape=jax.ShapeDtypeStruct((cell_devices, factors // cell_devices, width), bf),
+        out_shape=jax.ShapeDtypeStruct((factors // cell_devices, cell_devices * width), bf),
         in_specs=[
-            pl.BlockSpec(memory_space=pltpu.VMEM),
+            pl.BlockSpec(memory_space=pl.ANY),
             pl.BlockSpec(memory_space=pl.ANY),
             pl.BlockSpec(memory_space=pltpu.VMEM),
         ],
         out_specs=pl.BlockSpec(memory_space=pltpu.VMEM),
         scratch_shapes=[
+            vmem(activity_t.shape, bf),
             vmem((cell_devices, cells, width), bf),
             vmem((cell_devices, factors, width), bf),
             vmem((HOPS, Z_ROWS, width), bf),
@@ -776,7 +779,7 @@
             vmem((factors, width), f32),
             vmem((factors, width), bf),
             vmem((cell_devices, factors // cell_devices, width), bf),
-            dma((cell_devices,)),
+            dma, dma((cell_devices,)),
             dma((HOPS,)), dma((HOPS,)),
             dma((2,)), dma((2,)), dma((2, 2)), dma((2, 2)),
             dma((2,)), dma((2,)), dma((2,)), dma((2,)),
@@ -791,15 +794,13 @@
             collective_id=1, has_side_effects=True, vmem_limit_bytes=60 * 2**20
         ),
         name="solve",
-    )(activity_t, expression, relief)
+    )(activity_t, expression, block_mask)
 
 
 def on_device(expression, prior_values, block_mask, gram_inverse):
     activity_t = activity_of(expression, prior_values, block_mask, gram_inverse)
-    blocks = solve(activity_t, expression, block_mask)
-    rows = blocks.shape[1]
-    whole = blocks.transpose(1, 0, 2).reshape(rows, -1)
-    return whole[:, : expression.shape[1]].astype(jnp.float32)
+    rows = solve(activity_t, expression, block_mask)
+    return rows[:, : expression.shape[1]].astype(jnp.float32)
 
 
 def solution(mesh):

time: 163 us -> 161 us (0.988)
  local copies, waits for them, and re-layouts: 2.12 us -> 0 us
where the time goes in v6:
time: 161 us
  Pallas kernels  158 us (98%)
  other arithmetic  2.46 us (2%)
    pallas_call x1, Pallas kernels, solve(): pl.pallas_call(solve_kernel, out_shape=jax.ShapeDtypeStruct((factors // c...  86.7 us
    pallas_call x1, Pallas kernels, activity_of(): pl.pallas_call(activity_kernel, out_shape=jax.ShapeDtypeStruct((2, 4, 2,...  71.5 us

profile of v6, /device:TPU:1, one launch (start us, length us, event | category | flops | bytes accessed | tf_op | source)
XLA Modules:
  0.0 160.7 jit_solution(14222458503340999515)
XLA Ops:
  0.0 71.5 %activity.1.at_hbm = bf16[2,4,2,112,1024]{4,3,2,1,0:T(8,128)(2,1)} custom-call(bf16[1024,1920]{1,0:T(8,128)(2,1)} %x_hbm.3, bf16[1920,1792]{1,0:T(8,128)(2,1)} %prior_hbm.1, s32[15,14]{1,0:T(8,128)} %mask_ref.3, bf16[112,1792]{1,0:T(8,128)(2,1)} %bitcast.1), custom_call_target="tpu_custom_call" | custom-call | tf_op jit(solution)/shard_map/activity/pallas_call | solution.py:353
  71.5 86.7 %solve.1 = bf16[224,2048]{1,0:T(8,128)(2,1)} custom-call(bf16[2,4,2,112,1024]{4,3,2,1,0:T(8,128)(2,1)} %activity.1.at_hbm, bf16[1024,1920]{1,0:T(8,128)(2,1)} %x_hbm.3, s32[15,14]{1,0:T(8,128)} %mask_ref.3), custom_call_target="tpu_custom_call" | custom-call | tf_op jit(solution)/shard_map/solve/pallas_call | solution.py:750
  158.2 2.5 %slice_convert_fusion = f32[224,1920]{1,0:T(8,128)} fusion(bf16[224,2048]{1,0:T(8,128)(2,1)} %solve.1), kind=kLoop, calls=%fused_computation | loop fusion | flops 430080 | bytes 2580480 | tf_op jit(solution)/shard_map/convert_element_type | solution.py:803

commit v7 on v6

--- a/solution.py
+++ b/solution.py
@@ -17,8 +17,9 @@
 
 MESH = pl.DeviceIdType.MESH
 CHUNK = 256
+CUTS = (32, 80)
 SPLIT = 48
-LAGS = (0, 1, 4, 7, 11, 15, 16)
+LAGS = (0, 1, 5, 8, 12, 16, 17)
 
 
 class Spread:
@@ -100,6 +101,64 @@
                 self.hand_y(k, y_to, self.core).wait_send()
 
 
+class RelaySpread(Spread):
+    def relayed_by(self, cuts, send, recv):
+        self.near, self.far = self.ys[:2], self.ys[2][0]
+        self.halves = [(slice(r.start, c), slice(c, r.stop)) for r, c in zip(self.rows, cuts)]
+        self.w_send, self.w_recv = send, recv
+
+    def onward(self, k, j, slot):
+        zs = slice(None) if k else self.z
+        block = self.ref.at[zs, slot, self.core, self.halves[k][j]]
+        return self.remote(block, self.w_send.at[k, j], self.w_recv.at[k, j], self.near[j][1])
+
+    def forward(self, k):
+        for j in range(2):
+            slot, device = self.near[1 - j]
+            self.over_y(k, device, self.y, slot).wait_recv()
+            self.onward(k, j, slot).start()
+            self.hand_y(k, slot, self.core).start()
+
+    def from_far(self, k):
+        for j in range(2):
+            self.onward(k, j, self.far).wait_recv()
+        self.hand_y(k, self.far, self.core).start()
+
+    def run(self):
+        self.over_z(1, self.z).start()
+        for y_to, device in self.near:
+            self.over_y(0, device, y_to, self.y).start()
+        self.own(self.core).start()
+        self.forward(0)
+        self.over_z(1, 1 - self.z).wait_recv()
+        for y_to, device in self.near:
+            self.over_y(1, device, y_to, self.y).start()
+        self.hand_z(1, self.core).start()
+        self.from_far(0)
+        self.over_z(0, self.z).start()
+        self.forward(1)
+        self.from_far(1)
+        self.over_z(0, 1 - self.z).wait_recv()
+        self.hand_z(0, self.core).start()
+        self.own(1 - self.core).wait_recv()
+        for k in range(2):
+            self.hand_z(k, 1 - self.core).wait_recv()
+            for slot, _ in self.ys:
+                self.hand_y(k, slot, 1 - self.core).wait_recv()
+
+    def drain(self):
+        self.own(self.core).wait_send()
+        for k in range(2):
+            self.over_z(k, self.z).wait_send()
+            self.hand_z(k, self.core).wait_send()
+            for y_to, device in self.near:
+                self.over_y(k, device, y_to, self.y).wait_send()
+            for j in range(2):
+                self.onward(k, j, self.near[1 - j][0]).wait_send()
+            for y_to, _ in self.ys:
+                self.hand_y(k, y_to, self.core).wait_send()
+
+
 def activity_kernel(
     x_hbm, prior_hbm, mask_ref, gram_ref, at_ref,
     x, prior, support, part, pair, total, near_z, near_y, mid_z, mid_y, last_z, last_y, scores, acc,
@@ -107,7 +166,7 @@
     rs_y_send, rs_y_recv, rs_z_send, rs_z_recv,
     ag_y_send, ag_y_recv, ag_z_send, ag_z_recv, fw_send, fw_recv,
     at_y_send, at_y_recv, at_z_send, at_z_recv, own_send, own_recv,
-    af_y_send, af_y_recv, af_z_send, af_z_recv,
+    af_y_send, af_y_recv, af_z_send, af_z_recv, af_w_send, af_w_recv,
 ):
     chunks, genes, _ = prior.shape
     me = lax.axis_index("gene")
@@ -307,16 +366,14 @@
     lax.fori_loop(0, chunks + LAGS[-1], turn, 0)
 
     at_ref[z, y, core] = acc[...].astype(jnp.bfloat16)
-    spread_at = Spread(
+    spread_at = RelaySpread(
         at_ref, (z, y, core), slice(0, SPLIT), slice(SPLIT, at_ref.shape[3]),
         [(y_to, {"gene": device_of(y_to)}) for y_to in ys], {"gene": across}, {"gene": partner},
         (at_y_send, at_y_recv, at_z_send, at_z_recv, own_send, own_recv),
         (af_y_send, af_y_recv, af_z_send, af_z_recv),
     )
-    spread_at.begin()
-    spread_at.relay_high()
-    spread_at.relay_low()
-    spread_at.finish()
+    spread_at.relayed_by(CUTS, af_w_send, af_w_recv)
+    spread_at.run()
 
     def drain(n, carry):
         pair_copy(n).wait_send()
@@ -376,7 +433,7 @@
             dma((chunks, 4)), dma((chunks, 4)), dma((chunks,)), dma((chunks,)),
             dma((chunks,)), dma((chunks,)),
             dma((2, 4)), dma((2, 4)), dma((2,)), dma((2,)), dma, dma,
-            dma((2, 4)), dma((2, 4)), dma((2,)), dma((2,)),
+            dma((2, 4)), dma((2, 4)), dma((2,)), dma((2,)), dma((2, 2)), dma((2, 2)),
         ],
         compiler_params=pltpu.CompilerParams(
             collective_id=0, has_side_effects=True, vmem_limit_bytes=56 * 2**20

time: 161 us -> 160 us (level)
  no operation moved by 1% of the time
where the time goes in v7:
time: 160 us; the launch traced here: 159 us
  Pallas kernels  157 us (98%)
  other arithmetic  2.46 us (2%)
    pallas_call x1, Pallas kernels, solve(): pl.pallas_call(solve_kernel, out_shape=jax.ShapeDtypeStruct((factors // c...  86.6 us
    pallas_call x1, Pallas kernels, activity_of(): pl.pallas_call(activity_kernel, out_shape=jax.ShapeDtypeStruct((2, 4, 2,...  70.4 us

profile of v7, /device:TPU:1, one launch (start us, length us, event | category | flops | bytes accessed | tf_op | source)
XLA Modules:
  0.0 159.4 jit_solution(13062454775484527287)
XLA Ops:
  0.0 70.4 %activity.1.at_hbm = bf16[2,4,2,112,1024]{4,3,2,1,0:T(8,128)(2,1)} custom-call(bf16[1024,1920]{1,0:T(8,128)(2,1)} %x_hbm.3, bf16[1920,1792]{1,0:T(8,128)(2,1)} %prior_hbm.1, s32[15,14]{1,0:T(8,128)} %mask_ref.3, bf16[112,1792]{1,0:T(8,128)(2,1)} %bitcast.1), custom_call_target="tpu_custom_call" | custom-call | tf_op jit(solution)/shard_map/activity/pallas_call | solution.py:410
  70.4 86.6 %solve.1 = bf16[224,2048]{1,0:T(8,128)(2,1)} custom-call(bf16[2,4,2,112,1024]{4,3,2,1,0:T(8,128)(2,1)} %activity.1.at_hbm, bf16[1024,1920]{1,0:T(8,128)(2,1)} %x_hbm.3, s32[15,14]{1,0:T(8,128)} %mask_ref.3), custom_call_target="tpu_custom_call" | custom-call | tf_op jit(solution)/shard_map/solve/pallas_call | solution.py:807
  156.9 2.5 %slice_convert_fusion = f32[224,1920]{1,0:T(8,128)} fusion(bf16[224,2048]{1,0:T(8,128)(2,1)} %solve.1), kind=kLoop, calls=%fused_computation | loop fusion | flops 430080 | bytes 2580480 | tf_op jit(solution)/shard_map/convert_element_type | solution.py:860
